TPU v7x, 512 devices: a whole 4x4x16 slice. The times are simulated.
512 devices in a mesh: ctx: 64 (over z, x_lo, core), ch: 8 (over x_hi, y).
Axes of the slice: x: 4 (x_hi: 2, x_lo: 2; x = x_hi * 2 + x_lo), y: 4, z: 16, core: 2. Of those that a mesh axis runs over, the one named last changes fastest.
Arguments:
- q_in: bfloat16 [8192, 8192], P('ctx', 'ch'), may hold values from -6 to 6
- k_in: bfloat16 [8192, 8192], P('ctx', 'ch'), may hold values from -6 to 6
- v_in: bfloat16 [8192, 8192], P('ctx', 'ch'), may hold values from -6 to 6
- stretch_of_slot: int32 [128], replicated, may hold values from 0 to 127, each once
- short_weight: float32 [3, 7, 8192], P(None, None, 'ch'), may hold values from -2 to 2
- rates: float32 [16, 8192], P(None, 'ch'), may hold values from 1.2207031e-06 to 0.03
- residues: float32 [16, 8192], P(None, 'ch'), may hold values from -12 to 12
- skip: float32 [8192], P('ch'), may hold values from -4 to 4
- gain: float32 [8192], P('ch'), may hold values from 0.5 to 1.5
Outputs:
- operator_out: bfloat16 [8192, 8192], P('ctx', 'ch')
Inputs may be any that keep to these rules, and one draw needn't show every extreme that they name: stretch_of_slot names every sequence stretch exactly once.
All inputs are finite; a program needn't handle non-finite values.
Results may differ from a plain program's by a relative error of at most 0.001.
Values may be sent and summed in bfloat16 or wider, within the bound.
A program may use at most 64 MiB of HBM per device.

v0:
```python
import jax
import jax.numpy as jnp
from jax import lax
from jax.sharding import PartitionSpec as P

D = 8192


def decay_combine(earlier, later):
    return (earlier[0] * later[0], earlier[1] * later[0] + later[1])


def on_device(q_in, k_in, v_in, stretch_of_slot, short_weight, rates, residues, skip, gain):
    tokens, width = q_in.shape
    stretch = tokens // 2
    reach = short_weight.shape[1] - 1
    order = rates.shape[0]
    span = float(stretch)
    my_index = lax.axis_index("ctx")
    own_stretches = lax.dynamic_slice_in_dim(stretch_of_slot, 2 * my_index, 2)
    stacked = jnp.stack([q_in, k_in, v_in]).reshape(3, 2, stretch, width)
    tail_rows = (
        stacked[:, :, stretch - reach :, :].transpose(1, 0, 2, 3).reshape(2, 3 * reach, width)
    )
    stretch_ids = stretch_of_slot
    select = (stretch_ids[None, :] == own_stretches[:, None] - 1).astype(jnp.bfloat16)
    previous = jnp.einsum(
        "mn,nxw->mxw",
        select,
        lax.all_gather(tail_rows, "ctx", axis=0, tiled=True),
        preferred_element_type=jnp.float32,
    )
    previous = previous.reshape(2, 3, reach, width).transpose(1, 0, 2, 3)
    extended = jnp.concatenate([previous, stacked.astype(jnp.float32)], axis=2)
    features = jnp.zeros((3, 2, stretch, width), jnp.float32)
    for shift_by in range(reach + 1):
        features = (
            features
            + short_weight[:, shift_by][:, None, None, :]
            * extended[:, :, reach - shift_by : reach - shift_by + stretch, :]
        )
    query = features[0]
    mixed_in = features[1] * features[2]
    positions = jnp.arange(stretch, dtype=jnp.float32)
    scaled = residues * jnp.sqrt(-jnp.expm1(-2.0 * rates))

    def mode_pass(mode, state):
        local_conv, ends = state
        rate = lax.dynamic_index_in_dim(rates, mode, 0, keepdims=False)
        amount = lax.dynamic_index_in_dim(scaled, mode, 0, keepdims=False)
        factors = jnp.broadcast_to(jnp.exp(-rate)[None, None, :], mixed_in.shape)
        running = lax.associative_scan(decay_combine, (factors, mixed_in), axis=1)[1]
        local_conv = local_conv + amount[None, None, :] * running
        ends = lax.dynamic_update_index_in_dim(ends, running[:, stretch - 1 : stretch, :], mode, 1)
        return (local_conv, ends)

    local_conv, ends = lax.fori_loop(
        0,
        order,
        mode_pass,
        (jnp.zeros((2, stretch, width), jnp.float32), jnp.zeros((2, order, width), jnp.float32)),
    )
    pieces = lax.all_gather(ends, "ctx", axis=0, tiled=True)
    stretch_ids = stretch_of_slot

    def one_target(target):
        gaps = target - 1 - stretch_ids
        before = gaps >= 0
        steps_back = jnp.maximum(gaps, 0).astype(jnp.float32)
        weights = jnp.where(
            before[:, None, None], jnp.exp(-rates[None] * (span * steps_back[:, None, None])), 0.0
        )
        return jnp.sum(weights * pieces, axis=0)

    starts = lax.map(one_target, own_stretches)

    def carry_pass(mode, total):
        rate = lax.dynamic_index_in_dim(rates, mode, 0, keepdims=False)
        amount = lax.dynamic_index_in_dim(scaled, mode, 0, keepdims=False)
        lifted = jnp.exp(-rate[None, :] * (positions[:, None] + 1.0))
        begin = lax.dynamic_index_in_dim(starts, mode, 1, keepdims=False)
        return total + (amount[None, :] * lifted)[None] * begin[:, None, :]

    carried = lax.fori_loop(0, order, carry_pass, jnp.zeros((2, stretch, width), jnp.float32))
    output = local_conv + carried + skip[None, None, :] * mixed_in
    zvalues = query * output
    squares = lax.psum(jnp.sum(zvalues * zvalues, axis=-1), "ch")
    scale = lax.rsqrt(squares / D + 1e-05)
    normed = (zvalues * scale[:, :, None] * gain[None, None, :]).astype(jnp.bfloat16)
    return normed.reshape(tokens, width)


def solution(mesh):
    in_specs = (
        P("ctx", "ch"),
        P("ctx", "ch"),
        P("ctx", "ch"),
        P(),
        P(None, None, "ch"),
        P(None, "ch"),
        P(None, "ch"),
        P("ch"),
        P("ch"),
    )
    out_specs = P("ctx", "ch")
    return jax.shard_map(
        on_device, mesh=mesh, in_specs=in_specs, out_specs=out_specs, check_vma=False
    )
```

profile of v0, /device:TPU:1, one launch (start us, length us, event | category | flops | bytes accessed | tf_op | source)
XLA Modules:
  0.0 366.3 jit_solution(7288362771378136959)
XLA Ops:
  6.5 1.3 pad_maximum_fusion.6
  8.0 0.7 copy.21
  9.0 132.2 %all-gather.3.cloned.1.call-done = bf16[128,18,1024]{2,1,0:T(8,128)(2,1)} async-done(((bf16[2,18,1024]{2,1,0:T(8,128)(2,1)}), bf16[128,18,1024]{2,1,0:T(8,128)(2,1)}) %all-gather.3.cloned.1.call-update) | async-done | bytes 4718608 | tf_op jit(solution)/shard_map/all_gather | solution.py:30
  141.2 7.8 %fusion.8 = f32[2,18,1024]{2,0,1:T(2,128)S(1)} fusion(bf16[128,18,1024]{2,1,0:T(8,128)(2,1)} %all-gather.3.cloned.1.call-done, s32[128]{0:T(128)S(1)} %copy-done.8, s32[2]{0:T(128)S(1)} %get-tuple-element.404), kind=kOutput, calls=%fused_computation.44 | convolution fusion | flops 9437440 | bytes 4866568 | tf_op jit(solution)/shard_map/mn,nxw->mxw/dot_general | solution.py:27
  149.1 1.4 fusion.13
  150.5 1.2 copy-done
  151.8 43.7 %while.43 = (s32[]{:T(128)}, f32[2,64,1024]{2,1,0:T(8,128)S(1)}, f32[2,16,1024]{2,1,0:T(8,128)S(1)}, f32[16,1024]{1,0:T(8,128)S(1)}, f32[2,64,1024]{2,1,0:T(8,12...) while((s32[]{:T(128)}, f32[2,64,1024]{2,1,0:T(8,128)S(1)}, ...), condition=%wide.region_1.2_spmd.clone, body=%wide.region_0.1_spmd.clone.sunk | while | flops 1394691 | bytes 14254231 | solution.py:57
  154.2 0.3 select_add_fusion.4
  165.2 0.3 select_add_fusion.4
  167.9 0.3 select_add_fusion.4
  170.6 0.3 select_add_fusion.4
  173.4 0.3 select_add_fusion.4
  192.5 0.3 select_add_fusion.4
  195.2 0.3 select_add_fusion.4
  195.6 0.6 copy-done.2
  196.2 124.1 %all-gather.5.cloned.1.call-done = f32[128,16,1024]{2,1,0:T(8,128)} async-done(((f32[2,16,1024]{2,1,0:T(8,128)}), f32[128,16,1024]{2,1,0:T(8,128)}) %all-gather.5.cloned.1.call-update) | async-done | bytes 8388624 | tf_op jit(solution)/shard_map/all_gather | solution.py:63
  320.3 11.6 %while.42 = (s32[]{:T(128)}, f32[2,16,1024]{2,1,0:T(8,128)S(1)}, s32[2]{0:T(128)S(1)}, s32[128]{0:T(128)S(1)}, f32[1,16,1024]{2,1,0:T(8,128)S(1)}, /*index=5*/f32[128,16,1024]{2,1,0:T(8,128)}, s32[]{:T(128)}, s32[1]{0:T(128)}) while((s32[]{:T(128)}, f32[2,16,1024]{2,1,0:T(8,128)S(1)}, s32[2]{0:T(128)S(1)}, s32[128]{0:T(128)S(1)}, ...), condition=%wide.region_4.5_spmd, body=%wide.region_2.4_spmd.sunk | while | flops 8372995 | bytes 8653177 | solution.py:75
  320.3 0.6 dynamic_slice.66
  321.6 4.5 %multiply_reduce_fusion.3 = f32[16,1024]{1,0:T(8,128)S(1)} fusion(f32[128,16,1024]{2,1,0:T(8,128)} %get-tuple-element.615, f32[128]{0:T(128)S(1)} %convert_multiply_fusion.2, f32[16,1024]{1,0:T(8,128)S(1)} %bitcast.67, pred[128]{0:T(512)(128)(4,1)S(1)} %subtract_compare_fusion.2), kind=kLoop, calls=%fused_computation.1.clone.1 | loop fusion | flops 8372224 | bytes 8520320 | tf_op jit(solution)/shard_map/while/body/eval_jaxpr/reduce_sum | solution.py:73
  326.1 0.6 dynamic_slice.66
  327.4 4.5 %multiply_reduce_fusion.3 = f32[16,1024]{1,0:T(8,128)S(1)} fusion(f32[128,16,1024]{2,1,0:T(8,128)} %get-tuple-element.615, f32[128]{0:T(128)S(1)} %convert_multiply_fusion.2, f32[16,1024]{1,0:T(8,128)S(1)} %bitcast.67, pred[128]{0:T(512)(128)(4,1)S(1)} %subtract_compare_fusion.2), kind=kLoop, calls=%fused_computation.1.clone.1 | loop fusion | flops 8372224 | bytes 8520320 | tf_op jit(solution)/shard_map/while/body/eval_jaxpr/reduce_sum | solution.py:73
  331.9 6.2 %while.44 = (s32[]{:T(128)}, f32[2,64,1024]{2,1,0:T(8,128)S(1)}, f32[16,1024]{1,0:T(8,128)S(1)}, f32[16,1024]{1,0:T(8,128)S(1)}, f32[2,16,1024]{2,1,0:T(8,128)S(1)}, /*index=5*/s32[]{:T(128)}, s32[]{:T(128)}) while((s32[]{:T(128)}, f32[2,64,1024]{2,1,0:T(8,128)S(1)}, f32[16,1024]{1,0:T(8,128)S(1)}, f32[16,1024]{1,0:T(8,128)S(1)}, ...), condition=%wide.region_6.7_spmd.clone, body=%wide.region_5.6_spmd.clone.sunk | while | flops 525379 | bytes 1639007 | solution.py:84
  338.4 20.3 %psum.7 = f32[2,64]{1,0:T(2,128)S(1)} all-reduce(f32[2,64]{1,0:T(2,128)S(1)} %get-tuple-element.402), channel_id=1, replica_groups=mesh['ctx'=64,'ch'=8] {'ch'}, use_global_device_ids=true, to_apply=%region_8.9 | all-reduce | flops 128 | bytes 1024 | tf_op jit(solution)/shard_map/psum | solution.py:87
  358.7 0.8 multiply_convert_fusion
  (996 shorter events, 42.0 us)
Async XLA Ops:
  6.5 134.7 %all-gather.3.cloned.1.call-start = ((), (), s32[]{:S(2)}) async-start(), calls=%async_computation | async-start | bytes 6389760 | tf_op jit(solution)/shard_map/all_gather | solution.py:30
  6.5 2.2 copy-start.4
  6.5 2.3 copy-start.8
  6.5 2.4 copy-start.3
  6.5 2.4 copy-start.5
  8.7 311.6 %all-gather.5.cloned.1.call-start = ((), (), s32[]{:S(2)}) async-start(), calls=%async_computation.1 | async-start | bytes 8519680 | tf_op jit(solution)/shard_map/all_gather | solution.py:63
  150.5 1.2 copy-start
  195.6 0.7 copy-start.2
  331.9 6.2 %copy-start.1 = (f32[3,2,64,1024]{3,2,1,0:T(8,128)S(1)}, f32[3,2,64,1024]{3,2,1,0:T(8,128)}, u32[]{:S(2)}) copy-start(f32[3,2,64,1024]{3,2,1,0:T(8,128)} %copy-done) | copy-start | bytes 4718596
  331.9 6.2 %copy-start.6 = (f32[1024]{0:T(1024)S(1)}, f32[1024]{0:T(1024)}, u32[]{:S(2)}) copy-start(f32[1024]{0:T(1024)} %param.22) | copy-start | bytes 12292
  338.1 20.5 %copy-start.7 = (f32[1024]{0:T(1024)S(1)}, f32[1024]{0:T(1024)}, u32[]{:S(2)}) copy-start(f32[1024]{0:T(1024)} %param.23) | copy-start | bytes 12292
Sparse Core Ops, SparseCore 0:
  9.5 131.7 all-gather.2
  196.4 123.9 all-gather.4
where the time goes:
time: 369 us; the launch traced here: 366 us
  waiting for transfers between devices  256 us (69%)
  other arithmetic  30.7 us (8%)
  local copies, waits for them, and re-layouts  29.6 us (8%)
  blocking collectives  20.3 us (6%)
  between operations  13.6 us (4%)
  loops' own time  8.04 us (2%)
  matrix products  7.8 us (2%)
    all_gather x1, waiting for transfers between devices, on_device(): lax.all_gather(tail_rows, 'ctx', axis=0, tiled=True)  132 us
    all_gather x1, waiting for transfers between devices, on_device(): pieces = lax.all_gather(ends, 'ctx', axis=0, tiled=True)  124 us
    psum x1, blocking collectives, on_device(): squares = lax.psum(jnp.sum(zvalues * zvalues, axis=-1), 'ch')  20.3 us
    slice x288, local copies, waits for them, and re-layouts, mode_pass(): lax.associative_scan(decay_combine, (factors, mixed_in), axis=1)[1]  13.9 us
    pad x160, local copies, waits for them, and re-layouts, mode_pass(): lax.associative_scan(decay_combine, (factors, mixed_in), axis=1)[1]  9.36 us
    reduce_sum x2, other arithmetic, one_target(): return jnp.sum(weights * pieces, axis=0)  8.94 us
    dot_general x1, matrix products, on_device(): jnp.einsum('mn,nxw->mxw', select, lax.all_gather(tail_rows, 'ctx', axis=0...  7.8 us
  transfers between devices with their start and end apart: 2, of which 2 were waited for; matrix products, arithmetic and copies ran while one was open for 0% of the time, Pallas kernels for 0%

commit v1 on v0

v1 whole, which is shorter than its diff:
```python
import jax
import jax.numpy as jnp
from jax import lax
from jax.experimental import pallas as pl
from jax.experimental.pallas import tpu as pltpu
from jax.sharding import PartitionSpec as P

F32 = jnp.float32
BF16 = jnp.bfloat16
MESH = pl.DeviceIdType.MESH
HIGHEST = lax.Precision.HIGHEST

TOKENS = 128
WIDTH = 1024
STRETCH = 64
REACH = 6
TAPS = 7
ORDER = 16
OWNERS = 64
GROUP = 16
SLOTS = 128
EXT = STRETCH + REACH
PAD = 8
EPS = 1e-05


def iota(shape, dim):
    return lax.broadcasted_iota(jnp.int32, shape, dim)


def swap_groups(regs):
    regs = list(regs)
    group = iota((8, 128), 1) // GROUP
    for bit in (1, 2, 4):
        low = (group & bit) == 0
        for i in range(8):
            if i & bit:
                continue
            x, y = regs[i], regs[i | bit]
            regs[i] = jnp.where(low, x, pltpu.roll(y, GROUP * bit, 1))
            regs[i | bit] = jnp.where(low, pltpu.roll(x, 128 - GROUP * bit, 1), y)
    return regs


def one_minus_exp_neg(x):
    series = 1.0 - x / 9.0
    for n in (8, 7, 6, 5, 4, 3, 2):
        series = 1.0 - (x / n) * series
    return jnp.where(x < 0.3, x * series, 1.0 - jnp.exp(-x))


def kernel(
    n_ch,
    width_all,
    q_ref,
    k_ref,
    v_ref,
    sos_ref,
    sw_ref,
    rates_ref,
    res_ref,
    skip_ref,
    gain_ref,
    o_ref,
    ext,
    u_s,
    y_s,
    z_s,
    zn_s,
    rt,
    am,
    sw,
    filt,
    stage,
    own,
    six,
    pb,
    qt,
    pe,
    qs,
    mm,
    scan_s,
    sq_s,
    send_b,
    send_e,
    send_t,
    send_s,
    recv_b,
    recv_e,
    recv_t,
    recv_s,
    sq_send,
    sq_recv,
    ssem,
    rsem,
):
    me = lax.axis_index("ctx")
    my_ch = lax.axis_index("ch")
    my_z, my_l = me // 4, me % 4
    my_sub, my_lg = me // 8, me % 8

    barrier = pltpu.get_barrier_semaphore()

    @pl.loop(1, OWNERS)
    def _(i):
        pl.semaphore_signal(
            barrier, 1, device_id={"ctx": (me + i) % OWNERS}, device_id_type=MESH
        )

    @pl.loop(1, n_ch)
    def _(i):
        pl.semaphore_signal(
            barrier, 1, device_id={"ch": (my_ch + i) % n_ch}, device_id_type=MESH
        )

    def send_all(src, dst, sem):
        def one(d):
            pltpu.make_async_remote_copy(
                src_ref=src.at[d],
                dst_ref=dst.at[me],
                send_sem=ssem.at[sem],
                recv_sem=rsem.at[sem],
                device_id={"ctx": d},
                device_id_type=MESH,
            ).start()

        @pl.loop(0, 15)
        def _(i):
            step = 15 - i
            far = (step + 1) // 2
            d_z = (my_z + (2 * (step % 2) - 1) * far + 16) % 16
            for l in range(4):
                one(d_z * 4 + (my_l + l) % 4)

        for l in range(1, 4):
            one(my_z * 4 + (my_l + l) % 4)

    def all_of(src, dst, sem):
        return pltpu.make_async_remote_copy(
            src_ref=src.at[pl.ds(0, OWNERS - 1)],
            dst_ref=dst.at[pl.ds(0, OWNERS - 1)],
            send_sem=ssem.at[sem],
            recv_sem=rsem.at[sem],
            device_id={"ctx": (me + 1) % OWNERS},
            device_id_type=MESH,
        )

    def stage_to_send(dst):
        @pl.loop(0, 8)
        def _(b):
            for i in range(8):
                d = b * 8 + i
                dst[d] = stage[pl.ds(pl.multiple_of(d * 8, 8), 8), :].astype(BF16)

    def recv_to_stage(src):
        @pl.loop(0, 8)
        def _(b):
            for i in range(8):
                d = b * 8 + i
                stage[pl.ds(pl.multiple_of(d * 8, 8), 8), :] = src[d].astype(F32)

    def token(array, slot, t):
        return ext[array, pl.ds(pl.multiple_of((slot * EXT + REACH + t) * 8, 8), 8), :]

    def row8(ref, i):
        return ref[pl.ds(pl.multiple_of(i * 8, 8), 8), :]

    for array, ref in ((1, k_ref), (2, v_ref), (0, q_ref)):
        for slot in range(2):

            @pl.loop(0, 4)
            def _(tb):
                for j in range(8):
                    rows = ref[
                        pl.ds(pl.multiple_of(slot * STRETCH + tb * 16, 16), 16),
                        128 * j : 128 * j + 128,
                    ].astype(F32)
                    start = (slot * EXT + REACH + tb * 16) * 8 + j
                    ext[array, pl.ds(start, 16, stride=8), :] = rows

    for j in range(8):
        lanes = slice(128 * j, 128 * j + 128)
        rate = rates_ref[:, lanes]
        amount = res_ref[:, lanes] * jnp.sqrt(one_minus_exp_neg(2.0 * rate))
        rt[pl.ds(j, ORDER, stride=8), :] = rate
        am[pl.ds(j, ORDER, stride=8), :] = amount
        for a in range(3):
            sw[pl.ds(a * 64 + j, TAPS, stride=8), :] = sw_ref[a, :, lanes]
    for a in range(3):
        sw[a * 64 + 56 : a * 64 + 64, :] = jnp.zeros((8, 128), F32)

    for slot in range(2):
        kinds = (
            [token(1, slot, t) for t in range(6)] + [token(0, slot, 58), token(0, slot, 59)],
            [token(2, slot, t) for t in range(6)] + [token(0, slot, 60), token(0, slot, 61)],
            [token(0, slot, 62), token(0, slot, 63)] + [token(1, slot, 58 + t) for t in range(6)],
            [token(0, slot, 62), token(0, slot, 63)] + [token(2, slot, 58 + t) for t in range(6)],
        )
        for kind in range(4):
            for lg, reg in enumerate(swap_groups(kinds[kind])):
                stage[pl.ds(lg * 8 + slot * 4 + kind, 8, stride=64), :] = reg
    stage_to_send(send_b)

    def feature(array, slot, t):
        total = row8(sw, array * 8) * token(array, slot, t)
        for j in range(1, TAPS):
            total = total + row8(sw, array * 8 + j) * token(array, slot, t - j)
        return total

    def u_row(slot, t):
        return pl.ds(pl.multiple_of((slot * STRETCH + t) * 8, 8), 8)

    decay = [jnp.exp(-row8(rt, m)) for m in range(ORDER)]
    for slot in range(2):

        def step(t, acc):
            u = feature(1, slot, t) * feature(2, slot, t)
            u_s[u_row(slot, t), :] = u
            return tuple(a * d + u for a, d in zip(acc, decay))

        ends = lax.fori_loop(
            REACH, STRETCH, step, tuple(jnp.zeros((8, 128), F32) for _ in range(ORDER))
        )
        for h in range(2):
            for lg, reg in enumerate(swap_groups(ends[8 * h : 8 * h + 8])):
                hi = reg.astype(BF16).astype(F32)
                stage[pl.ds(lg * 8 + slot * 4 + 2 * h, 8, stride=64), :] = hi
                stage[pl.ds(lg * 8 + slot * 4 + 2 * h + 1, 8, stride=64), :] = reg - hi
    stage_to_send(send_e)

    pl.semaphore_wait(barrier, OWNERS - 1 + n_ch - 1)
    send_all(send_b, recv_b, 0)
    send_all(send_e, recv_e, 1)
    recv_b[me] = send_b[me]
    recv_e[me] = send_e[me]

    sos = jnp.broadcast_to(sos_ref[...].astype(F32), (SLOTS, SLOTS)).astype(BF16)
    spread = (iota((SLOTS, 512), 0) == iota((SLOTS, 512), 1) // 4).astype(F32).astype(BF16)
    sos_row = jnp.dot(sos[:16], spread, preferred_element_type=F32)[:1].astype(jnp.int32)
    spread_t = (iota((512, SLOTS), 1) == iota((512, SLOTS), 0) // 4).astype(F32).astype(BF16)
    scan_s[...] = lax.dot_general(
        spread_t, sos, (((1,), (1,)), ((), ())), preferred_element_type=F32
    )
    lane = iota((16, 512), 1)
    sublane = iota((16, 512), 0)
    sos_lane = jnp.broadcast_to(sos_row, (16, 512))

    @pl.loop(0, 32)
    def _(b):
        rows = pl.ds(pl.multiple_of(b * 16, 16), 16)
        row = sublane + b * 16
        here = scan_s[rows, :1].astype(jnp.int32)
        kind, s = row // SLOTS, row % SLOTS
        want = s - kind // 2
        hit = ((lane % 4) == kind) & (sos_lane == want)
        pb[rows, :] = hit.astype(F32).astype(BF16)
        hit = ((lane % 4) == row % 4) & (sos_lane == here - 1)
        qt[rows, :] = hit.astype(F32).astype(BF16)
        goal = (row % 2) * 256 + ((row % 4) // 2) * 128 + here - 1
        hit = (lane == goal) & (here > 0)
        qs[rows, :] = hit.astype(F32).astype(BF16)

    @pl.loop(0, 16)
    def _(b):
        rows = pl.ds(pl.multiple_of(b * 16, 16), 16)
        row = sublane + b * 16
        hit = ((lane % 4) // 2 == row // SLOTS) & (sos_lane == row % SLOTS)
        pe[rows, :] = hit.astype(F32).astype(BF16)

    own_rates = []
    for h in range(2):
        for lg, reg in enumerate(swap_groups([row8(rt, 8 * h + m) for m in range(8)])):
            own[lg * 8 : lg * 8 + 8, :] = reg
        own_rates.append(own[pl.ds(my_lg * 8 + my_sub, 1), :])

    lane128 = iota((8, 128), 1)

    def own_taps(array):
        rows = sw[pl.ds(array * 64 + my_sub, 8, stride=8), :]
        rows = pltpu.roll(rows, (128 - GROUP * my_lg) % 128, 1)
        rows = jnp.where(lane128 < GROUP, rows, 0.0)
        for shift in (16, 32, 64):
            rows = rows + pltpu.roll(rows, shift, 1)
        return rows

    taps_k, taps_v = own_taps(1), own_taps(2)
    r_row, r_lane = iota((128, 128), 0), iota((128, 128), 1)
    same = (r_row % GROUP == r_lane % GROUP) & (r_row // GROUP < REACH)
    ago = (STRETCH - 1 - r_row // GROUP).astype(F32)
    for h in range(2):
        mm[:, 128 * h : 128 * h + 128] = jnp.where(same, jnp.exp(-own_rates[h] * ago), 0.0)

    filt[0 : PAD * 8, :] = jnp.zeros((PAD * 8, 128), F32)

    def filter_step(d, powers):
        total = powers[0]
        for p in powers[1:]:
            total = total + p
        filt[pl.ds(pl.multiple_of((d + PAD) * 8, 8), 8), :] = total
        return tuple(p * x for p, x in zip(powers, decay))

    lax.fori_loop(0, STRETCH, filter_step, tuple(row8(am, m) for m in range(ORDER)))

    skip = skip_ref[...]

    @pl.loop(0, 8)
    def _(b):
        t0 = b * 8

        def inner(s, acc):
            taps = [row8(filt, t0 + i - s + PAD) for i in range(8)]
            out = []
            for slot in range(2):
                u = u_s[u_row(slot, s), :]
                out += [acc[slot * 8 + i] + taps[i] * u for i in range(8)]
            return tuple(out)

        acc = lax.fori_loop(
            REACH, t0 + 8, inner, tuple(jnp.zeros((8, 128), F32) for _ in range(16))
        )
        for slot in range(2):
            for i in range(8):
                y_s[u_row(slot, t0 + i), :] = acc[slot * 8 + i]

    for slot in range(2):

        @pl.loop(REACH, STRETCH)
        def _(t):
            z_s[u_row(slot, t), :] = feature(0, slot, t)
            rows = u_row(slot, t)
            y_s[rows, :] = y_s[rows, :] + skip * u_s[rows, :]

    all_of(send_b, recv_b, 0).wait_recv()
    recv_to_stage(recv_b)
    raw = stage[...].astype(BF16)
    stage[...] = jnp.dot(qt[...], raw, preferred_element_type=F32)
    stage_to_send(send_t)
    send_all(send_t, recv_t, 2)
    recv_t[me] = send_t[me]
    stage[...] = jnp.dot(pb[...], raw, preferred_element_type=F32)
    group16 = iota((16, 128), 1) // GROUP

    @pl.loop(0, 8)
    def _(b):
        def edge(kind, taps):
            head = stage[pl.ds(pl.multiple_of(kind * 128 + b * 16, 16), 16), :]
            tail = stage[pl.ds(pl.multiple_of(kind * 128 + 256 + b * 16, 16), 16), :]
            total = taps[0:1] * head
            for j in range(1, TAPS):
                mixed = jnp.where(group16 < 8 - j, head, tail)
                total = total + taps[j : j + 1] * pltpu.roll(mixed, GROUP * j, 1)
            return total

        six[pl.ds(pl.multiple_of(b * 16, 16), 16), :] = edge(0, taps_k) * edge(1, taps_v)

    extra = jnp.dot(six[...], mm[...], precision=HIGHEST, preferred_element_type=F32)

    all_of(send_e, recv_e, 1).wait_recv()
    recv_to_stage(recv_e)
    ends_seq = jnp.dot(pe[...], stage[...].astype(BF16), preferred_element_type=F32)
    sub8 = iota((8, 128), 0)
    for h in range(2):
        x = ends_seq[128 * h : 128 * h + 128] + extra[:, 128 * h : 128 * h + 128]
        span = own_rates[h] * float(STRETCH)
        blocks = [x[8 * b : 8 * b + 8] for b in range(16)]
        for d in (1, 2, 4):
            mult = jnp.where(sub8 >= d, jnp.exp(-span * float(d)), 0.0)
            blocks = [x + mult * pltpu.roll(x, d, 0) for x in blocks]
        lift = jnp.exp(-span * (sub8 + 1).astype(F32))
        whole = jnp.broadcast_to(jnp.exp(-span * 8.0), (8, 128))
        carry = jnp.zeros((8, 128), F32)
        for b in range(16):
            total = jnp.broadcast_to(blocks[b][7:8], (8, 128))
            done = blocks[b] + lift * carry
            carry = whole * carry + total
            hi = done.astype(BF16).astype(F32)
            scan_s[128 * h + 8 * b : 128 * h + 8 * b + 8, :] = hi
            scan_s[256 + 128 * h + 8 * b : 256 + 128 * h + 8 * b + 8, :] = done - hi
    stage[...] = jnp.dot(qs[...], scan_s[...].astype(BF16), preferred_element_type=F32)
    stage_to_send(send_s)
    send_all(send_s, recv_s, 3)
    recv_s[me] = send_s[me]

    all_of(send_t, recv_t, 2).wait_recv()
    recv_to_stage(recv_t)
    for slot in range(2):
        kinds = [
            swap_groups([stage[pl.ds(lg * 8 + slot * 4 + kind, 8, stride=64), :] for lg in range(8)])
            for kind in range(4)
        ]
        tails = (
            kinds[0][6:8] + kinds[1][6:8] + kinds[2][0:2],
            kinds[2][2:8],
            kinds[3][2:8],
        )
        for array in range(3):
            for t in range(6):
                base = (slot * EXT + t) * 8
                ext[array, base : base + 8, :] = tails[array][t]

    for slot in range(2):
        first = []
        for t in range(REACH):
            u = feature(1, slot, t) * feature(2, slot, t)
            first.append(u)
            z_s[u_row(slot, t), :] = feature(0, slot, t)
            rows = u_row(slot, t)
            y_s[rows, :] = y_s[rows, :] + skip * u

        @pl.loop(0, STRETCH)
        def _(t):
            rows = u_row(slot, t)
            total = y_s[rows, :]
            for s in range(REACH):
                total = total + row8(filt, t - s + PAD) * first[s]
            y_s[rows, :] = total

    all_of(send_s, recv_s, 3).wait_recv()
    recv_to_stage(recv_s)
    for slot in range(2):
        starts = []
        for h in range(2):
            base = slot * 4 + 2 * h
            starts += swap_groups(
                [
                    stage[pl.ds(lg * 8 + base, 8, stride=64), :]
                    + stage[pl.ds(lg * 8 + base + 1, 8, stride=64), :]
                    for lg in range(8)
                ]
            )

        def last(t, state):
            state = tuple(x * d for x, d in zip(state, decay))
            even, odd = state[0], state[1]
            for m in range(2, ORDER, 2):
                even, odd = even + state[m], odd + state[m + 1]
            rows = u_row(slot, t)
            z_s[rows, :] = z_s[rows, :] * (y_s[rows, :] + (even + odd))
            return state

        lax.fori_loop(
            0, STRETCH, last, tuple(s * row8(am, m) for m, s in enumerate(starts))
        )

    @pl.loop(0, 16)
    def _(b):
        rows = pl.ds(pl.multiple_of(b * 8, 8), 8)
        total = jnp.zeros((8, 128), F32)
        for j in range(8):
            z = z_s[pl.ds(b * 64 + j, 8, stride=8), :]
            zn_s[rows, 128 * j : 128 * j + 128] = z
            total = total + z * z
        sq_s[rows, :] = total

    sums = lax.dot_general(
        jnp.ones((8, 128), F32),
        sq_s[...],
        (((1,), (1,)), ((), ())),
        precision=HIGHEST,
        preferred_element_type=F32,
    )
    sq_send[0] = sums
    sq_recv[my_ch] = sums

    @pl.loop(1, n_ch)
    def _(i):
        pltpu.make_async_remote_copy(
            src_ref=sq_send.at[0],
            dst_ref=sq_recv.at[my_ch],
            send_sem=ssem.at[4],
            recv_sem=rsem.at[4],
            device_id={"ch": (my_ch + i) % n_ch},
            device_id_type=MESH,
        ).start()

    every = pltpu.make_async_remote_copy(
        src_ref=sq_recv.at[pl.ds(0, n_ch - 1)],
        dst_ref=sq_recv.at[pl.ds(0, n_ch - 1)],
        send_sem=ssem.at[4],
        recv_sem=rsem.at[4],
        device_id={"ch": (my_ch + 1) % n_ch},
        device_id_type=MESH,
    )
    every.wait_recv()
    total = sq_recv[0]
    for i in range(1, n_ch):
        total = total + sq_recv[i]
    scale = lax.rsqrt(total / float(width_all) + EPS)
    sq_s[...] = jnp.transpose(jnp.broadcast_to(scale[0:1], (128, 128)))

    @pl.loop(0, 8)
    def _(b):
        rows = pl.ds(pl.multiple_of(b * 16, 16), 16)
        by = sq_s[rows, :]
        for j in range(8):
            lanes = slice(128 * j, 128 * j + 128)
            o_ref[rows, lanes] = (zn_s[rows, lanes] * by * gain_ref[:, lanes]).astype(BF16)

    all_of(send_b, recv_b, 0).wait_send()
    all_of(send_e, recv_e, 1).wait_send()
    all_of(send_t, recv_t, 2).wait_send()
    all_of(send_s, recv_s, 3).wait_send()
    every.wait_send()


def on_device(n_ch, width_all, q_in, k_in, v_in, stretch_of_slot, short_weight, rates, residues, skip, gain):
    vmem = pl.BlockSpec(memory_space=pltpu.VMEM)
    f32 = lambda *shape: pltpu.VMEM(shape, F32)
    bf16 = lambda *shape: pltpu.VMEM(shape, BF16)
    scratch = (
        [f32(3, 2 * EXT * 8, 128)]
        + [f32(TOKENS * 8, 128)] * 3
        + [f32(TOKENS, WIDTH)]
        + [f32(ORDER * 8, 128)] * 2
        + [f32(192, 128), f32((STRETCH + PAD) * 8, 128), f32(512, 128), f32(64, 128), f32(128, 128)]
        + [bf16(512, 512), bf16(512, 512), bf16(256, 512), bf16(512, 512)]
        + [f32(128, 256), f32(512, 128), f32(128, 128)]
        + [bf16(OWNERS, 8, 128)] * 8
        + [f32(1, 8, 128), f32(n_ch, 8, 128)]
        + [pltpu.SemaphoreType.DMA((5,)), pltpu.SemaphoreType.DMA((5,))]
    )
    import functools

    return pl.pallas_call(
        functools.partial(kernel, n_ch, width_all),
        out_shape=jax.ShapeDtypeStruct((TOKENS, WIDTH), BF16),
        in_specs=[vmem] * 9,
        out_specs=vmem,
        scratch_shapes=scratch,
        compiler_params=pltpu.CompilerParams(collective_id=0, has_side_effects=True),
        name="hyena",
    )(
        q_in,
        k_in,
        v_in,
        stretch_of_slot.reshape(1, SLOTS),
        short_weight,
        rates,
        residues,
        skip.reshape(8, 128),
        gain.reshape(1, WIDTH),
    )


def solution(mesh):
    n_ch = mesh.shape["ch"]

    def body(*args):
        return on_device(n_ch, n_ch * WIDTH, *args)

    in_specs = (
        P("ctx", "ch"),
        P("ctx", "ch"),
        P("ctx", "ch"),
        P(),
        P(None, None, "ch"),
        P(None, "ch"),
        P(None, "ch"),
        P("ch"),
        P("ch"),
    )
    return jax.shard_map(
        body, mesh=mesh, in_specs=in_specs, out_specs=P("ctx", "ch"), check_vma=False
    )
```

time: 369 us -> 55.8 us (0.15)
  waiting for transfers between devices: 256 us -> 0 us
  Pallas kernels: 0 us -> 53.9 us
  other arithmetic: 30.7 us -> 0 us
  local copies, waits for them, and re-layouts: 29.6 us -> 1.67 us
  blocking collectives: 20.3 us -> 0 us
  between operations: 13.6 us -> 0.01 us
  loops' own time: 8.04 us -> 0 us
  matrix products: 7.8 us -> 0 us
    all_gather x2 -> x0, waiting for transfers between devices: 256 us -> none  [the longest x1 132 us: on_device(): lax.all_gather(tail_rows, 'ctx', axis=0, tiled=True)]
    pallas_call x0 -> x1, Pallas kernels: none -> 53.9 us  [on_device(): pl.pallas_call(functools.partial(kernel, n_ch, width_all), out_shape=jax....]
    psum x1 -> x0, blocking collectives: 20.3 us -> none  [on_device(): squares = lax.psum(jnp.sum(zvalues * zvalues, axis=-1), 'ch')]
    add x289 -> x0, other arithmetic: 14.2 us -> none  [the longest x16 4.92 us: mode_pass(): local_conv = local_conv + amount[None, None, :] * running]
    slice x289 -> x0, local copies, waits for them, and re-layouts: 14 us -> none  [the longest x288 13.9 us: mode_pass(): lax.associative_scan(decay_combine, (factors, mixed_in), axis=1)[1]]
    pad x160 -> x0, local copies, waits for them, and re-layouts: 9.36 us -> none  [mode_pass(): lax.associative_scan(decay_combine, (factors, mixed_in), axis=1)[1]]
    reduce_sum x3 -> x0, other arithmetic: 9.16 us -> none  [the longest x2 8.94 us: one_target(): return jnp.sum(weights * pieces, axis=0)]
    another operation x3 -> x0, loops' own time: 8.04 us -> none  [the longest x1 5.65 us: on_device(): lax.fori_loop(0, order, mode_pass, (jnp.zeros((2, stretch, width), jnp.fl...]
  transfers between devices with their start and end apart: 2 -> 0, of which waited for: 2 -> 0; matrix products, arithmetic and copies ran while one was open for 0% -> 0% of each run, Pallas kernels for 0% -> 0%
where the time goes in v1:
time: 55.8 us; the launch traced here: 55.6 us
  Pallas kernels  53.9 us (97%)
  local copies, waits for them, and re-layouts  1.67 us (3%)
    pallas_call x1, Pallas kernels, on_device(): pl.pallas_call(functools.partial(kernel, n_ch, width_all), out_shape=jax....  53.9 us
    unnamed x1, local copies, waits for them, and re-layouts  1.67 us

profile of v1, /device:TPU:1, one launch (start us, length us, event | category | flops | bytes accessed | tf_op | source)
XLA Modules:
  0.0 55.6 jit_solution(12596918504744188336)
XLA Ops:
  0.0 53.9 %hyena.1 = bf16[128,1024]{1,0:T(8,128)(2,1)} custom-call(bf16[128,1024]{1,0:T(8,128)(2,1)} %q_ref.1, bf16[128,1024]{1,0:T(8,128)(2,1)} %k_ref.1, bf16[128,1024]{1,0:T(8,128)(2,1)} %v_ref.1, s32[1,128]{1,0:T(1,128)} %bitcast.5, f32[3,7,1024]{2,1,0:T(8,128)} %sw_ref.1, f32[16,1024]{1,0:T(8,128)} %rates_ref.1, f32[16,1024]{1,0:T(8,128)} %res_ref.1, ...), custom_call_target="tpu_custom_call" | custom-call | tf_op jit(solution)/shard_map/hyena/pallas_call | solution.py:524
  53.9 1.7 %copy.11 = bf16[128,1024]{1,0:T(8,128)(2,1)} copy(bf16[128,1024]{1,0:T(8,128)(2,1)} %hyena.1) | data formatting | bytes 524288

commit v2 on v1

v2 whole, which is shorter than its diff:
```python
import functools

import jax
import jax.numpy as jnp
from jax import lax
from jax.experimental import pallas as pl
from jax.experimental.pallas import tpu as pltpu
from jax.sharding import PartitionSpec as P

F32 = jnp.float32
BF16 = jnp.bfloat16
MESH = pl.DeviceIdType.MESH
HIGHEST = lax.Precision.HIGHEST

TOKENS = 128
WIDTH = 1024
STRETCH = 64
REACH = 6
TAPS = 7
ORDER = 16
OWNERS = 64
GROUP = 16
SLOTS = 128
EXT = STRETCH + REACH
PAD = 8
EPS = 1e-05
FULL = 32000.0
TINY = 1e-30


def iota(shape, dim):
    return lax.broadcasted_iota(jnp.int32, shape, dim)


def swap_groups(regs):
    regs = list(regs)
    group = iota((8, 128), 1) // GROUP
    for bit in (1, 2, 4):
        low = (group & bit) == 0
        for i in range(8):
            if i & bit:
                continue
            x, y = regs[i], regs[i | bit]
            regs[i] = jnp.where(low, x, pltpu.roll(y, GROUP * bit, 1))
            regs[i | bit] = jnp.where(low, pltpu.roll(x, 128 - GROUP * bit, 1), y)
    return regs


def one_minus_exp_neg(x):
    series = 1.0 - x / 9.0
    for n in (8, 7, 6, 5, 4, 3, 2):
        series = 1.0 - (x / n) * series
    return jnp.where(x < 0.3, x * series, 1.0 - jnp.exp(-x))


def kernel(
    n_ch,
    width_all,
    q_hbm,
    k_hbm,
    v_hbm,
    sos_hbm,
    sw_hbm,
    rates_hbm,
    res_hbm,
    skip_hbm,
    gain_hbm,
    o_ref,
    q_ref,
    k_ref,
    v_ref,
    sos_ref,
    sw_ref,
    rates_ref,
    res_ref,
    skip_ref,
    gain_ref,
    ext,
    u_s,
    y_s,
    z_s,
    zn_s,
    rt,
    am,
    sw,
    filt,
    stage,
    own,
    six,
    pb,
    qt,
    pe,
    qs,
    mm,
    scan_s,
    scale_s,
    col_t,
    col_s,
    sq_s,
    send_b,
    send_t,
    recv_b,
    recv_t,
    send_e,
    send_s,
    recv_e,
    recv_s,
    send_x,
    recv_x,
    sq_send,
    sq_recv,
    ssem,
    rsem,
    isem,
):
    me = lax.axis_index("ctx")
    my_ch = lax.axis_index("ch")
    my_z, my_l = me // 4, me % 4
    my_sub, my_lg = me // 8, me % 8

    barrier = pltpu.get_barrier_semaphore()

    @pl.loop(1, OWNERS)
    def _(i):
        pl.semaphore_signal(
            barrier, 1, device_id={"ctx": (me + i) % OWNERS}, device_id_type=MESH
        )

    @pl.loop(1, n_ch)
    def _(i):
        pl.semaphore_signal(
            barrier, 1, device_id={"ch": (my_ch + i) % n_ch}, device_id_type=MESH
        )

    def load(i, src, dst):
        copy = pltpu.make_async_copy(src, dst, isem.at[i])
        copy.start()
        return copy

    loads = {
        "rates": load(0, rates_hbm, rates_ref),
        "res": load(1, res_hbm, res_ref),
        "sw": load(2, sw_hbm, sw_ref),
        "k": load(3, k_hbm, k_ref),
        "v": load(4, v_hbm, v_ref),
        "q": load(5, q_hbm, q_ref),
        "sos": load(6, sos_hbm, sos_ref),
        "skip": load(7, skip_hbm, skip_ref),
        "gain": load(8, gain_hbm, gain_ref),
    }

    def send_all(src, dst, sem):
        def one(d):
            pltpu.make_async_remote_copy(
                src_ref=src.at[d],
                dst_ref=dst.at[me],
                send_sem=ssem.at[sem],
                recv_sem=rsem.at[sem],
                device_id={"ctx": d},
                device_id_type=MESH,
            ).start()

        @pl.loop(0, 15)
        def _(i):
            step = 15 - i
            far = (step + 1) // 2
            d_z = (my_z + (2 * (step % 2) - 1) * far + 16) % 16
            for l in range(4):
                one(d_z * 4 + (my_l + l) % 4)

        for l in range(1, 4):
            one(my_z * 4 + (my_l + l) % 4)

    def all_of(src, dst, sem):
        return pltpu.make_async_remote_copy(
            src_ref=src.at[pl.ds(0, OWNERS - 1)],
            dst_ref=dst.at[pl.ds(0, OWNERS - 1)],
            send_sem=ssem.at[sem],
            recv_sem=rsem.at[sem],
            device_id={"ctx": (me + 1) % OWNERS},
            device_id_type=MESH,
        )

    def code(x):
        return x.astype(jnp.int32).astype(jnp.int16)

    def uncode(x):
        return x.astype(jnp.int32).astype(F32)

    def narrow(x):
        return x.astype(BF16)

    def widen(x):
        return x.astype(F32)

    def stage_to_send(dst, pitch, first, convert):
        rows = dst.shape[1]

        @pl.loop(0, 8)
        def _(b):
            for i in range(8):
                d = b * 8 + i
                dst[d] = convert(stage[pl.ds(d * pitch + first, rows), :])

    def recv_to_stage(src, pitch, first, convert):
        rows = src.shape[1]

        @pl.loop(0, 8)
        def _(b):
            for i in range(8):
                d = b * 8 + i
                stage[pl.ds(d * pitch + first, rows), :] = convert(src[d])

    def token(array, slot, t):
        return ext[array, pl.ds(pl.multiple_of((slot * EXT + REACH + t) * 8, 8), 8), :]

    def row8(ref, i):
        return ref[pl.ds(pl.multiple_of(i * 8, 8), 8), :]

    loads["rates"].wait()
    loads["res"].wait()
    loads["sw"].wait()
    for j in range(8):
        lanes = slice(128 * j, 128 * j + 128)
        rate = rates_ref[:, lanes]
        amount = res_ref[:, lanes] * jnp.sqrt(one_minus_exp_neg(2.0 * rate))
        rt[pl.ds(j, ORDER, stride=8), :] = rate
        am[pl.ds(j, ORDER, stride=8), :] = amount
        for a in range(3):
            sw[pl.ds(a * 64 + j, TAPS, stride=8), :] = sw_ref[a, :, lanes]
    for a in range(3):
        sw[a * 64 + 56 : a * 64 + 64, :] = jnp.zeros((8, 128), F32)

    for array, name, ref in ((1, "k", k_ref), (2, "v", v_ref), (0, "q", q_ref)):
        loads[name].wait()
        for slot in range(2):

            @pl.loop(0, 4)
            def _(tb):
                for j in range(8):
                    rows = ref[
                        pl.ds(pl.multiple_of(slot * STRETCH + tb * 16, 16), 16),
                        128 * j : 128 * j + 128,
                    ].astype(F32)
                    start = (slot * EXT + REACH + tb * 16) * 8 + j
                    ext[array, pl.ds(start, 16, stride=8), :] = rows
    loads["sos"].wait()
    loads["skip"].wait()
    loads["gain"].wait()

    def feature(array, slot, t):
        total = row8(sw, array * 8) * token(array, slot, t)
        for j in range(1, TAPS):
            total = total + row8(sw, array * 8 + j) * token(array, slot, t - j)
        return total

    def u_row(slot, t):
        return pl.ds(pl.multiple_of((slot * STRETCH + t) * 8, 8), 8)

    decay = [jnp.exp(-row8(rt, m)) for m in range(ORDER)]
    end_scale = []
    for slot in range(2):

        def step(t, acc):
            u = feature(1, slot, t) * feature(2, slot, t)
            u_s[u_row(slot, t), :] = u
            return tuple(a * d + u for a, d in zip(acc, decay))

        ends = lax.fori_loop(
            REACH,
            STRETCH,
            step,
            tuple(jnp.zeros((8, 128), F32) for _ in range(ORDER)),
            unroll=2,
        )
        largest = jnp.abs(ends[0])
        for end in ends[1:]:
            largest = jnp.maximum(largest, jnp.abs(end))
        scale = jnp.maximum(largest * 1.0078125, TINY).astype(BF16).astype(F32)
        end_scale.append(scale)
        inverse = FULL / scale
        ends = [jnp.round(end * inverse) for end in ends]
        for h in range(2):
            for lg, reg in enumerate(swap_groups(ends[8 * h : 8 * h + 8])):
                stage[pl.ds(lg * 4 + slot * 2 + h, 8, stride=32), :] = reg
    stage_to_send(send_e, 4, 0, code)

    for slot in range(2):
        q_tail = [token(0, slot, 58 + t) for t in range(6)]
        kinds = (
            [token(1, slot, t) for t in range(6)] + q_tail[0:2],
            [token(2, slot, t) for t in range(6)] + [end_scale[slot]] * 2,
            q_tail[4:6] + [token(1, slot, 58 + t) for t in range(6)],
            q_tail[2:4] + [token(2, slot, 58 + t) for t in range(6)],
        )
        for kind in range(4):
            for lg, reg in enumerate(swap_groups(kinds[kind])):
                stage[pl.ds(lg * 8 + slot * 4 + kind, 8, stride=64), :] = reg
    stage_to_send(send_b, 8, 0, narrow)

    pl.semaphore_wait(barrier, OWNERS - 1 + n_ch - 1)
    send_all(send_b, recv_b, 0)
    send_all(send_e, recv_e, 1)
    recv_b[me] = send_b[me]
    recv_e[me] = send_e[me]

    def ones_where(hit):
        return jnp.where(hit, 1.0, 0.0).astype(BF16)

    sos = jnp.broadcast_to(sos_ref[...].astype(F32), (SLOTS, SLOTS)).astype(BF16)
    spread = ones_where(iota((SLOTS, 512), 0) == (iota((SLOTS, 512), 1) >> 2))
    sos4 = jnp.dot(sos[:16], spread, preferred_element_type=F32)
    spread = ones_where(iota((SLOTS, 256), 0) == (iota((SLOTS, 256), 1) >> 1))
    sos2 = jnp.dot(sos[:16], spread, preferred_element_type=F32)
    across = (((1,), (1,)), ((), ()))
    row, lane = iota((512, SLOTS), 0), iota((512, SLOTS), 1)
    part = row & 7
    pair = (row >> 3) * 2
    slot_t = jnp.where(part >= 3, 1, 0)
    slot_s = jnp.where(part < 4, part >> 1, part & 1)
    col_t[...] = lax.dot_general(
        ones_where(lane == pair + slot_t), sos, across, preferred_element_type=F32
    )
    col_s[...] = lax.dot_general(
        ones_where(lane == pair + slot_s), sos, across, preferred_element_type=F32
    )
    lane, sublane = iota((16, 128), 1), iota((16, 128), 0)
    key4 = [
        sos4[:, 128 * c : 128 * c + 128].astype(jnp.int32) * 4 + (lane & 3) for c in range(4)
    ]
    key2 = [
        sos2[:, 128 * c : 128 * c + 128].astype(jnp.int32) * 2 + (lane & 1) for c in range(2)
    ]

    @pl.loop(0, 32)
    def _(b):
        rows = pl.ds(pl.multiple_of(b * 16, 16), 16)
        row = sublane + b * 16
        kind, s = row >> 7, row & 127
        want_b = (s - (kind >> 1)) * 4 + kind
        part = row & 7
        turn = jnp.where(part >= 3, part - 3, part)
        kind = jnp.where(turn > 0, turn + 1, turn)
        want_t = (col_t[rows, :].astype(jnp.int32) - 1) * 4 + kind
        want_t = jnp.where(part < 6, want_t, -1)
        before = col_s[rows, :].astype(jnp.int32) - 1
        want_s = before + jnp.where(part < 4, (part & 1) * 128, 256)
        want_s = jnp.where((part < 6) & (before >= 0), want_s, -1)
        for c in range(4):
            lanes = slice(128 * c, 128 * c + 128)
            pb[rows, lanes] = ones_where(key4[c] == want_b)
            qt[rows, lanes] = ones_where(key4[c] == want_t)
            if c < 3:
                qs[rows, lanes] = ones_where(lane + 128 * c == want_s)

    @pl.loop(0, 16)
    def _(b):
        rows = pl.ds(pl.multiple_of(b * 16, 16), 16)
        row = sublane + b * 16
        want = (row & 127) * 2 + (row >> 7)
        for c in range(2):
            pe[rows, 128 * c : 128 * c + 128] = ones_where(key2[c] == want)

    def own_modes(table):
        found = []
        for h in range(2):
            for lg, reg in enumerate(swap_groups([row8(table, 8 * h + m) for m in range(8)])):
                own[lg * 8 : lg * 8 + 8, :] = reg
            found.append(own[pl.ds(my_lg * 8 + my_sub, 1), :])
        return found

    own_rates, own_amounts = own_modes(rt), own_modes(am)

    lane128 = iota((8, 128), 1)

    def own_taps(array):
        rows = sw[pl.ds(array * 64 + my_sub, 8, stride=8), :]
        rows = pltpu.roll(rows, (128 - GROUP * my_lg) % 128, 1)
        rows = jnp.where(lane128 < GROUP, rows, 0.0)
        for shift in (16, 32, 64):
            rows = rows + pltpu.roll(rows, shift, 1)
        return rows

    taps_k, taps_v = own_taps(1), own_taps(2)
    r_row, r_lane = iota((128, 128), 0), iota((128, 128), 1)
    same = (r_row % GROUP == r_lane % GROUP) & (r_row // GROUP < REACH)
    ago = (STRETCH - 1 - r_row // GROUP).astype(F32)
    for h in range(2):
        mm[:, 128 * h : 128 * h + 128] = jnp.where(same, jnp.exp(-own_rates[h] * ago), 0.0)

    filt[0 : PAD * 8, :] = jnp.zeros((PAD * 8, 128), F32)

    def filter_step(d, powers):
        sums = list(powers)
        while len(sums) > 1:
            sums = [x + y for x, y in zip(sums[0::2], sums[1::2])]
        filt[pl.ds(pl.multiple_of((d + PAD) * 8, 8), 8), :] = sums[0]
        return tuple(p * x for p, x in zip(powers, decay))

    lax.fori_loop(
        0, STRETCH, filter_step, tuple(row8(am, m) for m in range(ORDER)), unroll=2
    )
    filt[PAD * 8 : PAD * 8 + 8, :] = filt[PAD * 8 : PAD * 8 + 8, :] + skip_ref[...]

    for slot in range(2):

        @pl.loop(REACH, STRETCH, unroll=2)
        def _(t):
            z_s[u_row(slot, t), :] = feature(0, slot, t)

    all_of(send_b, recv_b, 0).wait_recv()
    recv_to_stage(recv_b, 8, 0, widen)
    raw = stage[...].astype(BF16)
    stage[...] = jnp.dot(qt[...], raw, preferred_element_type=F32)
    stage_to_send(send_t, 8, 0, narrow)
    send_all(send_t, recv_t, 2)
    recv_t[me] = send_t[me]
    stage[...] = jnp.dot(pb[...], raw, preferred_element_type=F32)
    group16 = iota((16, 128), 1) // GROUP

    @pl.loop(0, 8)
    def _(b):
        def edge(kind, taps):
            head = stage[pl.ds(pl.multiple_of(kind * 128 + b * 16, 16), 16), :]
            tail = stage[pl.ds(pl.multiple_of(kind * 128 + 256 + b * 16, 16), 16), :]
            total = taps[0:1] * head
            for j in range(1, TAPS):
                mixed = jnp.where(group16 < 8 - j, head, tail)
                total = total + taps[j : j + 1] * pltpu.roll(mixed, GROUP * j, 1)
            return total

        rows = pl.ds(pl.multiple_of(b * 16, 16), 16)
        six[rows, :] = edge(0, taps_k) * edge(1, taps_v)
        scale = stage[pl.ds(pl.multiple_of(128 + b * 16, 16), 16), :] * (1.0 / FULL)
        scale = jnp.where(group16 == 6, scale, 0.0)
        for shift in (16, 32, 64):
            scale = scale + pltpu.roll(scale, shift, 1)
        scale_s[rows, :] = scale

    extra = jnp.dot(six[...], mm[...], precision=HIGHEST, preferred_element_type=F32)

    def halves(x):
        hi = jnp.floor(x * (1.0 / 256.0))
        return hi, x - 256.0 * hi

    all_of(send_e, recv_e, 1).wait_recv()
    recv_to_stage(recv_e, 4, 0, uncode)
    hi, lo = halves(stage[0:256, :])
    both = jnp.concatenate([hi.astype(BF16), lo.astype(BF16)], axis=1)
    both = jnp.dot(pe[...], both, preferred_element_type=F32)
    codes = both[:, :128] * 256.0 + both[:, 128:]
    sub8 = iota((8, 128), 0)
    states = []
    for h in range(2):
        x = codes[128 * h : 128 * h + 128] * scale_s[...] + extra[:, 128 * h : 128 * h + 128]
        span = own_rates[h] * float(STRETCH)
        blocks = [x[8 * b : 8 * b + 8] for b in range(16)]
        for d in (1, 2, 4):
            mult = jnp.where(sub8 >= d, jnp.exp(-span * float(d)), 0.0)
            blocks = [x + mult * pltpu.roll(x, d, 0) for x in blocks]
        lift = jnp.exp(-span * (sub8 + 1).astype(F32))
        whole = jnp.broadcast_to(jnp.exp(-span * 8.0), (8, 128))
        carry = jnp.zeros((8, 128), F32)
        done = []
        for b in range(16):
            total = jnp.broadcast_to(blocks[b][7:8], (8, 128))
            done.append((blocks[b] + lift * carry) * own_amounts[h])
            carry = whole * carry + total
        states.append(done)
    for b in range(16):
        x0, x1 = states[0][b], states[1][b]
        largest = jnp.maximum(jnp.abs(x0), jnp.abs(x1))
        for shift in (16, 32, 64):
            largest = jnp.maximum(largest, pltpu.roll(largest, shift, 1))
        power = jnp.ceil(jnp.log2(jnp.maximum(largest, TINY)))
        inverse = jnp.exp2(-power) * FULL
        for h, x in enumerate((x0, x1)):
            hi, lo = halves(jnp.round(x * inverse))
            scan_s[128 * h + 8 * b : 128 * h + 8 * b + 8, 0:128] = hi
            scan_s[128 * h + 8 * b : 128 * h + 8 * b + 8, 128:256] = lo
        scan_s[256 + 8 * b : 256 + 8 * b + 8, 0:128] = jnp.zeros((8, 128), F32)
        scan_s[256 + 8 * b : 256 + 8 * b + 8, 128:256] = power
    both = jnp.dot(qs[...], scan_s[...].astype(BF16), preferred_element_type=F32)
    stage[...] = both[:, :128] * 256.0 + both[:, 128:]
    stage_to_send(send_s, 8, 0, code)
    stage_to_send(send_x, 8, 4, code)
    send_all(send_s, recv_s, 3)
    send_all(send_x, recv_x, 5)
    recv_s[me] = send_s[me]
    recv_x[me] = send_x[me]

    for b in range(8):
        t0 = b * 8

        def inner(s, acc):
            taps = [row8(filt, t0 + i - s + PAD) for i in range(8)]
            out = []
            for slot in range(2):
                u = u_s[u_row(slot, s), :]
                out += [acc[slot * 8 + i] + taps[i] * u for i in range(8)]
            return tuple(out)

        acc = lax.fori_loop(
            REACH,
            t0 + 8,
            inner,
            tuple(jnp.zeros((8, 128), F32) for _ in range(16)),
            unroll=2,
        )
        for slot in range(2):
            for i in range(8):
                y_s[u_row(slot, t0 + i), :] = acc[slot * 8 + i]

    all_of(send_t, recv_t, 2).wait_recv()
    recv_to_stage(recv_t, 8, 0, widen)
    for slot in range(2):
        kinds = [
            swap_groups(
                [stage[pl.ds(lg * 8 + slot * 3 + turn, 8, stride=64), :] for lg in range(8)]
            )
            for turn in range(3)
        ]
        tails = (
            kinds[0][6:8] + kinds[2][0:2] + kinds[1][0:2],
            kinds[1][2:8],
            kinds[2][2:8],
        )
        for array in range(3):
            for t in range(6):
                base = (slot * EXT + t) * 8
                ext[array, base : base + 8, :] = tails[array][t]

    for slot in range(2):
        first = []
        for t in range(REACH):
            first.append(feature(1, slot, t) * feature(2, slot, t))
            z_s[u_row(slot, t), :] = feature(0, slot, t)

        @pl.loop(0, STRETCH, unroll=2)
        def _(t):
            rows = u_row(slot, t)
            total = y_s[rows, :]
            for s in range(REACH):
                total = total + row8(filt, t - s + PAD) * first[s]
            y_s[rows, :] = total

    all_of(send_s, recv_s, 3).wait_recv()
    recv_to_stage(recv_s, 8, 0, uncode)
    all_of(send_x, recv_x, 5).wait_recv()
    recv_to_stage(recv_x, 8, 4, uncode)
    for slot in range(2):
        scales = [
            jnp.exp2(stage[pl.ds(lg * 8 + 4 + slot, 8, stride=64), :]) * (1.0 / FULL)
            for lg in range(8)
        ]
        starts = []
        for h in range(2):
            starts += swap_groups(
                [
                    stage[pl.ds(lg * 8 + slot * 2 + h, 8, stride=64), :] * scales[lg]
                    for lg in range(8)
                ]
            )

        def last(t, state):
            state = tuple(x * d for x, d in zip(state, decay))
            sums = list(state)
            while len(sums) > 1:
                sums = [x + y for x, y in zip(sums[0::2], sums[1::2])]
            rows = u_row(slot, t)
            z_s[rows, :] = z_s[rows, :] * (y_s[rows, :] + sums[0])
            return state

        lax.fori_loop(0, STRETCH, last, tuple(starts), unroll=2)

    @pl.loop(0, 16)
    def _(b):
        rows = pl.ds(pl.multiple_of(b * 8, 8), 8)
        total = jnp.zeros((8, 128), F32)
        for j in range(8):
            z = z_s[pl.ds(b * 64 + j, 8, stride=8), :]
            zn_s[rows, 128 * j : 128 * j + 128] = z
            total = total + z * z
        sq_s[rows, :] = total

    sums = lax.dot_general(
        jnp.ones((8, 128), F32),
        sq_s[...],
        (((1,), (1,)), ((), ())),
        precision=HIGHEST,
        preferred_element_type=F32,
    )
    sq_send[0] = sums
    sq_recv[my_ch] = sums

    @pl.loop(1, n_ch)
    def _(i):
        pltpu.make_async_remote_copy(
            src_ref=sq_send.at[0],
            dst_ref=sq_recv.at[my_ch],
            send_sem=ssem.at[4],
            recv_sem=rsem.at[4],
            device_id={"ch": (my_ch + i) % n_ch},
            device_id_type=MESH,
        ).start()

    every = pltpu.make_async_remote_copy(
        src_ref=sq_recv.at[pl.ds(0, n_ch - 1)],
        dst_ref=sq_recv.at[pl.ds(0, n_ch - 1)],
        send_sem=ssem.at[4],
        recv_sem=rsem.at[4],
        device_id={"ch": (my_ch + 1) % n_ch},
        device_id_type=MESH,
    )
    every.wait_recv()
    total = sq_recv[0]
    for i in range(1, n_ch):
        total = total + sq_recv[i]
    scale = lax.rsqrt(total / float(width_all) + EPS)
    sq_s[...] = jnp.transpose(jnp.broadcast_to(scale[0:1], (128, 128)))

    @pl.loop(0, 8)
    def _(b):
        rows = pl.ds(pl.multiple_of(b * 16, 16), 16)
        by = sq_s[rows, :]
        for j in range(8):
            lanes = slice(128 * j, 128 * j + 128)
            o_ref[rows, lanes] = (zn_s[rows, lanes] * by * gain_ref[:, lanes]).astype(BF16)

    all_of(send_b, recv_b, 0).wait_send()
    all_of(send_e, recv_e, 1).wait_send()
    all_of(send_t, recv_t, 2).wait_send()
    all_of(send_s, recv_s, 3).wait_send()
    all_of(send_x, recv_x, 5).wait_send()
    every.wait_send()


def on_device(n_ch, width_all, q_in, k_in, v_in, stretch_of_slot, short_weight, rates, residues, skip, gain):
    vmem = pl.BlockSpec(memory_space=pltpu.VMEM)
    hbm = pl.BlockSpec(memory_space=pltpu.HBM)
    f32 = lambda *shape: pltpu.VMEM(shape, F32)
    bf16 = lambda *shape: pltpu.VMEM(shape, BF16)
    i16 = lambda *shape: pltpu.VMEM(shape, jnp.int16)
    scratch = (
        [bf16(TOKENS, WIDTH)] * 3
        + [pltpu.VMEM((1, SLOTS), jnp.int32), f32(3, TAPS, WIDTH)]
        + [f32(ORDER, WIDTH)] * 2
        + [f32(8, 128), f32(1, WIDTH)]
        + [f32(3, 2 * EXT * 8, 128)]
        + [f32(TOKENS * 8, 128)] * 3
        + [f32(TOKENS, WIDTH)]
        + [f32(ORDER * 8, 128)] * 2
        + [f32(192, 128), f32((STRETCH + PAD) * 8, 128), f32(512, 128), f32(64, 128), f32(128, 128)]
        + [bf16(512, 512), bf16(512, 512), bf16(256, 256), bf16(512, 384)]
        + [f32(128, 256), f32(384, 256), f32(128, 128), f32(512, 128), f32(512, 128), f32(128, 128)]
        + [bf16(OWNERS, 8, 128)] * 4
        + [i16(OWNERS, 4, 128)] * 4
        + [i16(OWNERS, 2, 128)] * 2
        + [f32(1, 8, 128), f32(n_ch, 8, 128)]
        + [pltpu.SemaphoreType.DMA((6,)), pltpu.SemaphoreType.DMA((6,))]
        + [pltpu.SemaphoreType.DMA((9,))]
    )
    return pl.pallas_call(
        functools.partial(kernel, n_ch, width_all),
        out_shape=jax.ShapeDtypeStruct((TOKENS, WIDTH), BF16),
        in_specs=[hbm] * 9,
        out_specs=vmem,
        scratch_shapes=scratch,
        compiler_params=pltpu.CompilerParams(collective_id=0, has_side_effects=True),
        name="hyena",
    )(
        q_in,
        k_in,
        v_in,
        stretch_of_slot.reshape(1, SLOTS),
        short_weight,
        rates,
        residues,
        skip.reshape(8, 128),
        gain.reshape(1, WIDTH),
    )


def solution(mesh):
    n_ch = mesh.shape["ch"]

    def body(*args):
        return on_device(n_ch, n_ch * WIDTH, *args)

    in_specs = (
        P("ctx", "ch"),
        P("ctx", "ch"),
        P("ctx", "ch"),
        P(),
        P(None, None, "ch"),
        P(None, "ch"),
        P(None, "ch"),
        P("ch"),
        P("ch"),
    )
    return jax.shard_map(
        body, mesh=mesh, in_specs=in_specs, out_specs=P("ctx", "ch"), check_vma=False
    )
```

time: 55.8 us -> 54.2 us (0.971)
  Pallas kernels: 53.9 us -> 52.4 us
    pallas_call x1, Pallas kernels: 53.9 us -> 52.4 us  [on_device(): pl.pallas_call(functools.partial(kernel, n_ch, width_all), out_shape=jax....]
where the time goes in v2:
time: 54.2 us; the launch traced here: 54.1 us
  Pallas kernels  52.4 us (97%)
  local copies, waits for them, and re-layouts  1.67 us (3%)
    pallas_call x1, Pallas kernels, on_device(): pl.pallas_call(functools.partial(kernel, n_ch, width_all), out_shape=jax....  52.4 us
    unnamed x1, local copies, waits for them, and re-layouts  1.67 us

profile of v2, /device:TPU:1, one launch (start us, length us, event | category | flops | bytes accessed | tf_op | source)
XLA Modules:
  0.0 54.1 jit_solution(8069226183273368727)
XLA Ops:
  0.0 52.4 %hyena.1 = bf16[128,1024]{1,0:T(8,128)(2,1)} custom-call(bf16[128,1024]{1,0:T(8,128)(2,1)} %q_hbm.1, bf16[128,1024]{1,0:T(8,128)(2,1)} %k_hbm.1, bf16[128,1024]{1,0:T(8,128)(2,1)} %v_hbm.1, s32[1,128]{1,0:T(1,128)} %bitcast.5, f32[3,7,1024]{2,1,0:T(8,128)} %sw_hbm.1, f32[16,1024]{1,0:T(8,128)} %rates_hbm.1, f32[16,1024]{1,0:T(8,128)} %res_hbm.1, ...), custom_call_target="tpu_custom_call" | custom-call | tf_op jit(solution)/shard_map/hyena/pallas_call | solution.py:663
  52.4 1.7 %copy.11 = bf16[128,1024]{1,0:T(8,128)(2,1)} copy(bf16[128,1024]{1,0:T(8,128)(2,1)} %hyena.1) | data formatting | bytes 524288

commit v3 on v2

--- a/solution.py
+++ b/solution.py
@@ -21,7 +21,6 @@
 OWNERS = 64
 GROUP = 16
 SLOTS = 128
-EXT = STRETCH + REACH
 PAD = 8
 EPS = 1e-05
 FULL = 32000.0
@@ -88,25 +87,23 @@
     own,
     six,
     pb,
-    qt,
     pe,
     qs,
     mm,
+    m1,
+    extra,
+    rows_s,
+    codes_s,
     scan_s,
     scale_s,
-    col_t,
     col_s,
     sq_s,
     send_b,
-    send_t,
     recv_b,
-    recv_t,
     send_e,
+    recv_e,
     send_s,
-    recv_e,
     recv_s,
-    send_x,
-    recv_x,
     sq_send,
     sq_recv,
     ssem,
@@ -212,7 +209,7 @@
                 stage[pl.ds(d * pitch + first, rows), :] = convert(src[d])
 
     def token(array, slot, t):
-        return ext[array, pl.ds(pl.multiple_of((slot * EXT + REACH + t) * 8, 8), 8), :]
+        return ext[array, pl.ds(pl.multiple_of((slot * STRETCH + t) * 8, 8), 8), :]
 
     def row8(ref, i):
         return ref[pl.ds(pl.multiple_of(i * 8, 8), 8), :]
@@ -242,7 +239,7 @@
                         pl.ds(pl.multiple_of(slot * STRETCH + tb * 16, 16), 16),
                         128 * j : 128 * j + 128,
                     ].astype(F32)
-                    start = (slot * EXT + REACH + tb * 16) * 8 + j
+                    start = (slot * STRETCH + tb * 16) * 8 + j
                     ext[array, pl.ds(start, 16, stride=8), :] = rows
     loads["sos"].wait()
     loads["skip"].wait()
@@ -288,9 +285,9 @@
     for slot in range(2):
         q_tail = [token(0, slot, 58 + t) for t in range(6)]
         kinds = (
-            [token(1, slot, t) for t in range(6)] + q_tail[0:2],
+            [token(1, slot, t) for t in range(6)] + q_tail[4:6],
             [token(2, slot, t) for t in range(6)] + [end_scale[slot]] * 2,
-            q_tail[4:6] + [token(1, slot, 58 + t) for t in range(6)],
+            q_tail[0:2] + [token(1, slot, 58 + t) for t in range(6)],
             q_tail[2:4] + [token(2, slot, 58 + t) for t in range(6)],
         )
         for kind in range(4):
@@ -313,17 +310,8 @@
     spread = ones_where(iota((SLOTS, 256), 0) == (iota((SLOTS, 256), 1) >> 1))
     sos2 = jnp.dot(sos[:16], spread, preferred_element_type=F32)
     across = (((1,), (1,)), ((), ()))
-    row, lane = iota((512, SLOTS), 0), iota((512, SLOTS), 1)
-    part = row & 7
-    pair = (row >> 3) * 2
-    slot_t = jnp.where(part >= 3, 1, 0)
-    slot_s = jnp.where(part < 4, part >> 1, part & 1)
-    col_t[...] = lax.dot_general(
-        ones_where(lane == pair + slot_t), sos, across, preferred_element_type=F32
-    )
-    col_s[...] = lax.dot_general(
-        ones_where(lane == pair + slot_s), sos, across, preferred_element_type=F32
-    )
+    spread = ones_where(iota((512, SLOTS), 1) == (iota((512, SLOTS), 0) >> 2))
+    col_s[...] = lax.dot_general(spread, sos, across, preferred_element_type=F32)
     lane, sublane = iota((16, 128), 1), iota((16, 128), 0)
     key4 = [
         sos4[:, 128 * c : 128 * c + 128].astype(jnp.int32) * 4 + (lane & 3) for c in range(4)
@@ -332,26 +320,21 @@
         sos2[:, 128 * c : 128 * c + 128].astype(jnp.int32) * 2 + (lane & 1) for c in range(2)
     ]
 
+    @pl.loop(0, 40)
+    def _(b):
+        rows = pl.ds(pl.multiple_of(b * 16, 16), 16)
+        row = sublane + b * 16
+        block = row >> 7
+        want = ((row & 127) - jnp.where(block >= 2, 1, 0)) * 4 + (block & 3)
+        for c in range(4):
+            pb[rows, 128 * c : 128 * c + 128] = ones_where(key4[c] == want)
+
     @pl.loop(0, 32)
     def _(b):
         rows = pl.ds(pl.multiple_of(b * 16, 16), 16)
-        row = sublane + b * 16
-        kind, s = row >> 7, row & 127
-        want_b = (s - (kind >> 1)) * 4 + kind
-        part = row & 7
-        turn = jnp.where(part >= 3, part - 3, part)
-        kind = jnp.where(turn > 0, turn + 1, turn)
-        want_t = (col_t[rows, :].astype(jnp.int32) - 1) * 4 + kind
-        want_t = jnp.where(part < 6, want_t, -1)
-        before = col_s[rows, :].astype(jnp.int32) - 1
-        want_s = before + jnp.where(part < 4, (part & 1) * 128, 256)
-        want_s = jnp.where((part < 6) & (before >= 0), want_s, -1)
+        want = (sublane & 3) * 128 + col_s[rows, :].astype(jnp.int32)
         for c in range(4):
-            lanes = slice(128 * c, 128 * c + 128)
-            pb[rows, lanes] = ones_where(key4[c] == want_b)
-            qt[rows, lanes] = ones_where(key4[c] == want_t)
-            if c < 3:
-                qs[rows, lanes] = ones_where(lane + 128 * c == want_s)
+            qs[rows, 128 * c : 128 * c + 128] = ones_where(lane + 128 * c == want)
 
     @pl.loop(0, 16)
     def _(b):
@@ -361,6 +344,32 @@
         for c in range(2):
             pe[rows, 128 * c : 128 * c + 128] = ones_where(key2[c] == want)
 
+    filt[0 : PAD * 8, :] = jnp.zeros((PAD * 8, 128), F32)
+
+    def filter_step(d, powers):
+        sums = list(powers)
+        while len(sums) > 1:
+            sums = [x + y for x, y in zip(sums[0::2], sums[1::2])]
+        filt[pl.ds(pl.multiple_of((d + PAD) * 8, 8), 8), :] = sums[0]
+        return tuple(p * x for p, x in zip(powers, decay))
+
+    lax.fori_loop(
+        0, STRETCH, filter_step, tuple(row8(am, m) for m in range(ORDER)), unroll=2
+    )
+    filt[PAD * 8 : PAD * 8 + 8, :] = filt[PAD * 8 : PAD * 8 + 8, :] + skip_ref[...]
+
+    for slot in range(2):
+
+        for t in range(REACH):
+            total = row8(sw, 0) * token(0, slot, t)
+            for j in range(1, t + 1):
+                total = total + row8(sw, j) * token(0, slot, t - j)
+            z_s[u_row(slot, t), :] = total
+
+        @pl.loop(REACH, STRETCH, unroll=2)
+        def _(t):
+            z_s[u_row(slot, t), :] = feature(0, slot, t)
+
     def own_modes(table):
         found = []
         for h in range(2):
@@ -373,75 +382,91 @@
 
     lane128 = iota((8, 128), 1)
 
-    def own_taps(array):
-        rows = sw[pl.ds(array * 64 + my_sub, 8, stride=8), :]
+    def own_taps(table, first):
+        rows = table[pl.ds(first + my_sub, 8, stride=8), :]
         rows = pltpu.roll(rows, (128 - GROUP * my_lg) % 128, 1)
         rows = jnp.where(lane128 < GROUP, rows, 0.0)
         for shift in (16, 32, 64):
             rows = rows + pltpu.roll(rows, shift, 1)
         return rows
 
-    taps_k, taps_v = own_taps(1), own_taps(2)
+    taps_q, taps_k, taps_v = own_taps(sw, 0), own_taps(sw, 64), own_taps(sw, 128)
+    own_filter = own_taps(filt, PAD * 8)
     r_row, r_lane = iota((128, 128), 0), iota((128, 128), 1)
-    same = (r_row % GROUP == r_lane % GROUP) & (r_row // GROUP < REACH)
-    ago = (STRETCH - 1 - r_row // GROUP).astype(F32)
+    same = (r_row & (GROUP - 1)) == (r_lane & (GROUP - 1))
+    g_row, g_lane = r_row >> 4, r_lane >> 4
+    inside = same & (g_row < REACH)
     for h in range(2):
-        mm[:, 128 * h : 128 * h + 128] = jnp.where(same, jnp.exp(-own_rates[h] * ago), 0.0)
-
-    filt[0 : PAD * 8, :] = jnp.zeros((PAD * 8, 128), F32)
-
-    def filter_step(d, powers):
-        sums = list(powers)
-        while len(sums) > 1:
-            sums = [x + y for x, y in zip(sums[0::2], sums[1::2])]
-        filt[pl.ds(pl.multiple_of((d + PAD) * 8, 8), 8), :] = sums[0]
-        return tuple(p * x for p, x in zip(powers, decay))
-
-    lax.fori_loop(
-        0, STRETCH, filter_step, tuple(row8(am, m) for m in range(ORDER)), unroll=2
-    )
-    filt[PAD * 8 : PAD * 8 + 8, :] = filt[PAD * 8 : PAD * 8 + 8, :] + skip_ref[...]
-
-    for slot in range(2):
-
-        @pl.loop(REACH, STRETCH, unroll=2)
-        def _(t):
-            z_s[u_row(slot, t), :] = feature(0, slot, t)
+        lift = jnp.exp(-own_rates[h] * (REACH - 1 - g_row).astype(F32))
+        mm[:, 128 * h : 128 * h + 128] = jnp.where(inside, lift, 0.0)
+        rate = jnp.transpose(jnp.broadcast_to(own_rates[h], (128, 128)))
+        lift = jnp.exp(-rate * (g_lane + 1).astype(F32))
+        lift = jnp.where(same & (g_lane < REACH), lift, 0.0)
+        upper = lift.astype(BF16)
+        lower = (lift - upper.astype(F32)).astype(BF16)
+        for i, part in enumerate((upper, lower, upper)):
+            m1[256 * i + 128 * h : 256 * i + 128 * h + 128, :] = part
+    near = jnp.zeros((128, 128), F32)
+    inside = inside & (g_lane < REACH)
+    for d in range(REACH):
+        near = jnp.where(inside & (g_lane - g_row == d), own_filter[d : d + 1], near)
+    mm[:, 256:384] = near
+
+    def halves(x):
+        hi = jnp.floor(x * (1.0 / 256.0))
+        return hi, x - 256.0 * hi
+
+    def group_max(x):
+        for shift in (16, 32, 64):
+            x = jnp.maximum(x, pltpu.roll(x, shift, 1))
+        return x
+
+    def power_of(largest):
+        return jnp.ceil(jnp.log2(jnp.maximum(largest, TINY)))
+
+    def encode(x, power):
+        return jnp.round(x * (jnp.exp2(-power) * FULL))
+
+    def put(kind, rows, x):
+        hi, lo = halves(x)
+        at = pl.ds(kind * 128 + rows, x.shape[0])
+        codes_s[at, 0:128] = hi.astype(BF16)
+        codes_s[at, 128:256] = lo.astype(BF16)
 
     all_of(send_b, recv_b, 0).wait_recv()
     recv_to_stage(recv_b, 8, 0, widen)
-    raw = stage[...].astype(BF16)
-    stage[...] = jnp.dot(qt[...], raw, preferred_element_type=F32)
-    stage_to_send(send_t, 8, 0, narrow)
-    send_all(send_t, recv_t, 2)
-    recv_t[me] = send_t[me]
-    stage[...] = jnp.dot(pb[...], raw, preferred_element_type=F32)
-    group16 = iota((16, 128), 1) // GROUP
+    rows_s[...] = jnp.dot(pb[...], stage[...].astype(BF16), preferred_element_type=F32)
+    group = iota((16, 128), 1) >> 4
 
     @pl.loop(0, 8)
     def _(b):
-        def edge(kind, taps):
-            head = stage[pl.ds(pl.multiple_of(kind * 128 + b * 16, 16), 16), :]
-            tail = stage[pl.ds(pl.multiple_of(kind * 128 + 256 + b * 16, 16), 16), :]
+        first = pl.multiple_of(b * 16, 16)
+
+        def block(kind):
+            return rows_s[pl.ds(pl.multiple_of(kind * 128 + b * 16, 16), 16), :]
+
+        def edge(head, tail, taps):
             total = taps[0:1] * head
             for j in range(1, TAPS):
-                mixed = jnp.where(group16 < 8 - j, head, tail)
+                mixed = jnp.where(group < 8 - j, head, tail)
                 total = total + taps[j : j + 1] * pltpu.roll(mixed, GROUP * j, 1)
             return total
 
-        rows = pl.ds(pl.multiple_of(b * 16, 16), 16)
-        six[rows, :] = edge(0, taps_k) * edge(1, taps_v)
-        scale = stage[pl.ds(pl.multiple_of(128 + b * 16, 16), 16), :] * (1.0 / FULL)
-        scale = jnp.where(group16 == 6, scale, 0.0)
+        rows = pl.ds(first, 16)
+        head_v, tail_k, tail_v = block(1), block(2), block(3)
+        six[rows, :] = edge(block(0), tail_k, taps_k) * edge(head_v, tail_v, taps_v)
+        scale = jnp.where(group == 6, head_v * (1.0 / FULL), 0.0)
         for shift in (16, 32, 64):
             scale = scale + pltpu.roll(scale, shift, 1)
         scale_s[rows, :] = scale
-
-    extra = jnp.dot(six[...], mm[...], precision=HIGHEST, preferred_element_type=F32)
-
-    def halves(x):
-        hi = jnp.floor(x * (1.0 / 256.0))
-        return hi, x - 256.0 * hi
+        tail_q = jnp.where(group >= 4, pltpu.roll(tail_v, 64, 1), pltpu.roll(tail_k, 32, 1))
+        tail_q = jnp.where(group >= 6, block(4), tail_q)
+        part = edge(jnp.zeros_like(tail_q), tail_q, taps_q)
+        part = jnp.where(group < REACH, part, 0.0)
+        power = power_of(group_max(jnp.abs(part)))
+        put(3, first, jnp.where(group == 6, power, encode(part, power)))
+
+    extra[...] = jnp.dot(six[...], mm[...], precision=HIGHEST, preferred_element_type=F32)
 
     all_of(send_e, recv_e, 1).wait_recv()
     recv_to_stage(recv_e, 4, 0, uncode)
@@ -450,9 +475,10 @@
     both = jnp.dot(pe[...], both, preferred_element_type=F32)
     codes = both[:, :128] * 256.0 + both[:, 128:]
     sub8 = iota((8, 128), 0)
-    states = []
     for h in range(2):
-        x = codes[128 * h : 128 * h + 128] * scale_s[...] + extra[:, 128 * h : 128 * h + 128]
+        lanes = slice(128 * h, 128 * h + 128)
+        late = jnp.exp(-own_rates[h] * float(STRETCH - REACH))
+        x = codes[128 * h : 128 * h + 128] * scale_s[...] + extra[:, lanes] * late
         span = own_rates[h] * float(STRETCH)
         blocks = [x[8 * b : 8 * b + 8] for b in range(16)]
         for d in (1, 2, 4):
@@ -461,33 +487,40 @@
         lift = jnp.exp(-span * (sub8 + 1).astype(F32))
         whole = jnp.broadcast_to(jnp.exp(-span * 8.0), (8, 128))
         carry = jnp.zeros((8, 128), F32)
-        done = []
+        scan_s[h, 0:8, :] = carry
         for b in range(16):
             total = jnp.broadcast_to(blocks[b][7:8], (8, 128))
-            done.append((blocks[b] + lift * carry) * own_amounts[h])
+            scan_s[h, 8 * b + 1 : 8 * b + 9, :] = blocks[b] + lift * carry
             carry = whole * carry + total
-        states.append(done)
-    for b in range(16):
-        x0, x1 = states[0][b], states[1][b]
-        largest = jnp.maximum(jnp.abs(x0), jnp.abs(x1))
-        for shift in (16, 32, 64):
-            largest = jnp.maximum(largest, pltpu.roll(largest, shift, 1))
-        power = jnp.ceil(jnp.log2(jnp.maximum(largest, TINY)))
-        inverse = jnp.exp2(-power) * FULL
-        for h, x in enumerate((x0, x1)):
-            hi, lo = halves(jnp.round(x * inverse))
-            scan_s[128 * h + 8 * b : 128 * h + 8 * b + 8, 0:128] = hi
-            scan_s[128 * h + 8 * b : 128 * h + 8 * b + 8, 128:256] = lo
-        scan_s[256 + 8 * b : 256 + 8 * b + 8, 0:128] = jnp.zeros((8, 128), F32)
-        scan_s[256 + 8 * b : 256 + 8 * b + 8, 128:256] = power
-    both = jnp.dot(qs[...], scan_s[...].astype(BF16), preferred_element_type=F32)
+    start = [scan_s[h, 0:128, :] * own_amounts[h] for h in range(2)]
+    wide = jnp.concatenate(start, axis=1)
+    upper = wide.astype(BF16)
+    lower = (wide - upper.astype(F32)).astype(BF16)
+    wide = jnp.concatenate([upper, upper, lower], axis=1)
+    rows_s[0:128, :] = extra[:, 256:384] + jnp.dot(
+        wide, m1[...], preferred_element_type=F32
+    )
+    late = [
+        start[h] * jnp.exp(-own_rates[h] * float(REACH))
+        + extra[:, 128 * h : 128 * h + 128] * own_amounts[h]
+        for h in range(2)
+    ]
+    for b in range(8):
+        rows = slice(16 * b, 16 * b + 16)
+        power = power_of(
+            group_max(jnp.maximum(jnp.abs(late[0][rows]), jnp.abs(late[1][rows])))
+        )
+        for h in range(2):
+            put(h, 16 * b, encode(late[h][rows], power))
+        y = rows_s[rows, :]
+        power_y = power_of(group_max(jnp.abs(y)))
+        y = jnp.where(group == 6, power, jnp.where(group == 7, power_y, encode(y, power_y)))
+        put(2, 16 * b, y)
+    both = jnp.dot(qs[...], codes_s[...], preferred_element_type=F32)
     stage[...] = both[:, :128] * 256.0 + both[:, 128:]
     stage_to_send(send_s, 8, 0, code)
-    stage_to_send(send_x, 8, 4, code)
-    send_all(send_s, recv_s, 3)
-    send_all(send_x, recv_x, 5)
+    send_all(send_s, recv_s, 2)
     recv_s[me] = send_s[me]
-    recv_x[me] = send_x[me]
 
     for b in range(8):
         t0 = b * 8
@@ -511,56 +544,22 @@
             for i in range(8):
                 y_s[u_row(slot, t0 + i), :] = acc[slot * 8 + i]
 
-    all_of(send_t, recv_t, 2).wait_recv()
-    recv_to_stage(recv_t, 8, 0, widen)
+    all_of(send_s, recv_s, 2).wait_recv()
+    recv_to_stage(recv_s, 8, 0, uncode)
     for slot in range(2):
-        kinds = [
+        low, high, y_part, q_part = [
             swap_groups(
-                [stage[pl.ds(lg * 8 + slot * 3 + turn, 8, stride=64), :] for lg in range(8)]
+                [stage[pl.ds(lg * 8 + slot * 4 + kind, 8, stride=64), :] for lg in range(8)]
             )
-            for turn in range(3)
+            for kind in range(4)
         ]
-        tails = (
-            kinds[0][6:8] + kinds[2][0:2] + kinds[1][0:2],
-            kinds[1][2:8],
-            kinds[2][2:8],
-        )
-        for array in range(3):
-            for t in range(6):
-                base = (slot * EXT + t) * 8
-                ext[array, base : base + 8, :] = tails[array][t]
-
-    for slot in range(2):
-        first = []
+        scale = jnp.exp2(y_part[6]) * (1.0 / FULL)
+        scale_y = jnp.exp2(y_part[7]) * (1.0 / FULL)
+        scale_q = jnp.exp2(q_part[6]) * (1.0 / FULL)
         for t in range(REACH):
-            first.append(feature(1, slot, t) * feature(2, slot, t))
-            z_s[u_row(slot, t), :] = feature(0, slot, t)
-
-        @pl.loop(0, STRETCH, unroll=2)
-        def _(t):
             rows = u_row(slot, t)
-            total = y_s[rows, :]
-            for s in range(REACH):
-                total = total + row8(filt, t - s + PAD) * first[s]
-            y_s[rows, :] = total
-
-    all_of(send_s, recv_s, 3).wait_recv()
-    recv_to_stage(recv_s, 8, 0, uncode)
-    all_of(send_x, recv_x, 5).wait_recv()
-    recv_to_stage(recv_x, 8, 4, uncode)
-    for slot in range(2):
-        scales = [
-            jnp.exp2(stage[pl.ds(lg * 8 + 4 + slot, 8, stride=64), :]) * (1.0 / FULL)
-            for lg in range(8)
-        ]
-        starts = []
-        for h in range(2):
-            starts += swap_groups(
-                [
-                    stage[pl.ds(lg * 8 + slot * 2 + h, 8, stride=64), :] * scales[lg]
-                    for lg in range(8)
-                ]
-            )
+            query = z_s[rows, :] + q_part[t] * scale_q
+            z_s[rows, :] = query * (y_part[t] * scale_y)
 
         def last(t, state):
             state = tuple(x * d for x, d in zip(state, decay))
@@ -571,7 +570,9 @@
             z_s[rows, :] = z_s[rows, :] * (y_s[rows, :] + sums[0])
             return state
 
-        lax.fori_loop(0, STRETCH, last, tuple(starts), unroll=2)
+        lax.fori_loop(
+            REACH, STRETCH, last, tuple(x * scale for x in low + high), unroll=2
+        )
 
     @pl.loop(0, 16)
     def _(b):
@@ -598,8 +599,8 @@
         pltpu.make_async_remote_copy(
             src_ref=sq_send.at[0],
             dst_ref=sq_recv.at[my_ch],
-            send_sem=ssem.at[4],
-            recv_sem=rsem.at[4],
+            send_sem=ssem.at[3],
+            recv_sem=rsem.at[3],
             device_id={"ch": (my_ch + i) % n_ch},
             device_id_type=MESH,
         ).start()
@@ -607,8 +608,8 @@
     every = pltpu.make_async_remote_copy(
         src_ref=sq_recv.at[pl.ds(0, n_ch - 1)],
         dst_ref=sq_recv.at[pl.ds(0, n_ch - 1)],
-        send_sem=ssem.at[4],
-        recv_sem=rsem.at[4],
+        send_sem=ssem.at[3],
+        recv_sem=rsem.at[3],
         device_id={"ch": (my_ch + 1) % n_ch},
         device_id_type=MESH,
     )
@@ -629,9 +630,7 @@
 
     all_of(send_b, recv_b, 0).wait_send()
     all_of(send_e, recv_e, 1).wait_send()
-    all_of(send_t, recv_t, 2).wait_send()
-    all_of(send_s, recv_s, 3).wait_send()
-    all_of(send_x, recv_x, 5).wait_send()
+    all_of(send_s, recv_s, 2).wait_send()
     every.wait_send()
 
 
@@ -646,18 +645,19 @@
         + [pltpu.VMEM((1, SLOTS), jnp.int32), f32(3, TAPS, WIDTH)]
         + [f32(ORDER, WIDTH)] * 2
         + [f32(8, 128), f32(1, WIDTH)]
-        + [f32(3, 2 * EXT * 8, 128)]
+        + [f32(3, TOKENS * 8, 128)]
         + [f32(TOKENS * 8, 128)] * 3
         + [f32(TOKENS, WIDTH)]
         + [f32(ORDER * 8, 128)] * 2
         + [f32(192, 128), f32((STRETCH + PAD) * 8, 128), f32(512, 128), f32(64, 128), f32(128, 128)]
-        + [bf16(512, 512), bf16(512, 512), bf16(256, 256), bf16(512, 384)]
-        + [f32(128, 256), f32(384, 256), f32(128, 128), f32(512, 128), f32(512, 128), f32(128, 128)]
-        + [bf16(OWNERS, 8, 128)] * 4
-        + [i16(OWNERS, 4, 128)] * 4
-        + [i16(OWNERS, 2, 128)] * 2
+        + [bf16(640, 512), bf16(256, 256), bf16(512, 512)]
+        + [f32(128, 384), bf16(768, 128), f32(128, 384), f32(640, 128), bf16(512, 256)]
+        + [f32(2, 136, 128), f32(128, 128), f32(512, 128), f32(128, 128)]
+        + [bf16(OWNERS, 8, 128)] * 2
+        + [i16(OWNERS, 4, 128)] * 2
+        + [i16(OWNERS, 8, 128)] * 2
         + [f32(1, 8, 128), f32(n_ch, 8, 128)]
-        + [pltpu.SemaphoreType.DMA((6,)), pltpu.SemaphoreType.DMA((6,))]
+        + [pltpu.SemaphoreType.DMA((4,)), pltpu.SemaphoreType.DMA((4,))]
         + [pltpu.SemaphoreType.DMA((9,))]
     )
     return pl.pallas_call(

time: 54.2 us -> 52.5 us (0.969)
  Pallas kernels: 52.4 us -> 50.6 us
    pallas_call x1, Pallas kernels: 52.4 us -> 50.6 us  [on_device(): pl.pallas_call(functools.partial(kernel, n_ch, width_all), out_shape=jax....]
where the time goes in v3:
time: 52.5 us; the launch traced here: 52.3 us
  Pallas kernels  50.6 us (96%)
  local copies, waits for them, and re-layouts  1.67 us (3%)
    pallas_call x1, Pallas kernels, on_device(): pl.pallas_call(functools.partial(kernel, n_ch, width_all), out_shape=jax....  50.6 us
    unnamed x1, local copies, waits for them, and re-layouts  1.67 us

profile of v3, /device:TPU:1, one launch (start us, length us, event | category | flops | bytes accessed | tf_op | source)
XLA Modules:
  0.0 52.3 jit_solution(1386931140152878919)
XLA Ops:
  0.0 50.6 %hyena.1 = bf16[128,1024]{1,0:T(8,128)(2,1)} custom-call(bf16[128,1024]{1,0:T(8,128)(2,1)} %q_hbm.1, bf16[128,1024]{1,0:T(8,128)(2,1)} %k_hbm.1, bf16[128,1024]{1,0:T(8,128)(2,1)} %v_hbm.1, s32[1,128]{1,0:T(1,128)} %bitcast.5, f32[3,7,1024]{2,1,0:T(8,128)} %sw_hbm.1, f32[16,1024]{1,0:T(8,128)} %rates_hbm.1, f32[16,1024]{1,0:T(8,128)} %res_hbm.1, ...), custom_call_target="tpu_custom_call" | custom-call | tf_op jit(solution)/shard_map/hyena/pallas_call | solution.py:663
  50.7 1.7 %copy.11 = bf16[128,1024]{1,0:T(8,128)(2,1)} copy(bf16[128,1024]{1,0:T(8,128)(2,1)} %hyena.1) | data formatting | bytes 524288

commit v4 on v3

--- a/solution.py
+++ b/solution.py
@@ -86,9 +86,9 @@
     stage,
     own,
     six,
-    pb,
-    pe,
-    qs,
+    gather,
+    scatter,
+    powers,
     mm,
     m1,
     extra,
@@ -96,7 +96,6 @@
     codes_s,
     scan_s,
     scale_s,
-    col_s,
     sq_s,
     send_b,
     recv_b,
@@ -304,45 +303,13 @@
     def ones_where(hit):
         return jnp.where(hit, 1.0, 0.0).astype(BF16)
 
-    sos = jnp.broadcast_to(sos_ref[...].astype(F32), (SLOTS, SLOTS)).astype(BF16)
-    spread = ones_where(iota((SLOTS, 512), 0) == (iota((SLOTS, 512), 1) >> 2))
-    sos4 = jnp.dot(sos[:16], spread, preferred_element_type=F32)
-    spread = ones_where(iota((SLOTS, 256), 0) == (iota((SLOTS, 256), 1) >> 1))
-    sos2 = jnp.dot(sos[:16], spread, preferred_element_type=F32)
-    across = (((1,), (1,)), ((), ()))
-    spread = ones_where(iota((512, SLOTS), 1) == (iota((512, SLOTS), 0) >> 2))
-    col_s[...] = lax.dot_general(spread, sos, across, preferred_element_type=F32)
-    lane, sublane = iota((16, 128), 1), iota((16, 128), 0)
-    key4 = [
-        sos4[:, 128 * c : 128 * c + 128].astype(jnp.int32) * 4 + (lane & 3) for c in range(4)
-    ]
-    key2 = [
-        sos2[:, 128 * c : 128 * c + 128].astype(jnp.int32) * 2 + (lane & 1) for c in range(2)
-    ]
-
-    @pl.loop(0, 40)
-    def _(b):
-        rows = pl.ds(pl.multiple_of(b * 16, 16), 16)
-        row = sublane + b * 16
-        block = row >> 7
-        want = ((row & 127) - jnp.where(block >= 2, 1, 0)) * 4 + (block & 3)
-        for c in range(4):
-            pb[rows, 128 * c : 128 * c + 128] = ones_where(key4[c] == want)
-
-    @pl.loop(0, 32)
-    def _(b):
-        rows = pl.ds(pl.multiple_of(b * 16, 16), 16)
-        want = (sublane & 3) * 128 + col_s[rows, :].astype(jnp.int32)
-        for c in range(4):
-            qs[rows, 128 * c : 128 * c + 128] = ones_where(lane + 128 * c == want)
-
-    @pl.loop(0, 16)
-    def _(b):
-        rows = pl.ds(pl.multiple_of(b * 16, 16), 16)
-        row = sublane + b * 16
-        want = (row & 127) * 2 + (row >> 7)
-        for c in range(2):
-            pe[rows, 128 * c : 128 * c + 128] = ones_where(key2[c] == want)
+    sos_row = jnp.broadcast_to(sos_ref[...], (16, SLOTS))
+    sublane = iota((16, SLOTS), 0)
+    for b in range(16):
+        s = sublane + (16 * b - (129 if b >= 8 else 0))
+        gather[16 * b : 16 * b + 16, :] = ones_where(sos_row == s)
+    sos_column = jnp.transpose(jnp.broadcast_to(sos_ref[...].astype(F32), (SLOTS, SLOTS)))
+    scatter[...] = ones_where(sos_column.astype(jnp.int32) == iota((SLOTS, SLOTS), 1))
 
     filt[0 : PAD * 8, :] = jnp.zeros((PAD * 8, 128), F32)
 
@@ -396,21 +363,40 @@
     same = (r_row & (GROUP - 1)) == (r_lane & (GROUP - 1))
     g_row, g_lane = r_row >> 4, r_lane >> 4
     inside = same & (g_row < REACH)
+
+    def split(x):
+        upper = x.astype(BF16)
+        return upper, (x - upper.astype(F32)).astype(BF16)
+
+    def put_mm(part, x):
+        lanes = slice(128 * part, 128 * part + 128)
+        mm[0:128, lanes], mm[128:256, lanes] = split(x)
+        mm[256:384, lanes] = mm[0:128, lanes]
+
     for h in range(2):
         lift = jnp.exp(-own_rates[h] * (REACH - 1 - g_row).astype(F32))
-        mm[:, 128 * h : 128 * h + 128] = jnp.where(inside, lift, 0.0)
+        put_mm(h, jnp.where(inside, lift, 0.0))
         rate = jnp.transpose(jnp.broadcast_to(own_rates[h], (128, 128)))
         lift = jnp.exp(-rate * (g_lane + 1).astype(F32))
         lift = jnp.where(same & (g_lane < REACH), lift, 0.0)
-        upper = lift.astype(BF16)
-        lower = (lift - upper.astype(F32)).astype(BF16)
+        upper, lower = split(lift)
         for i, part in enumerate((upper, lower, upper)):
             m1[256 * i + 128 * h : 256 * i + 128 * h + 128, :] = part
     near = jnp.zeros((128, 128), F32)
     inside = inside & (g_lane < REACH)
     for d in range(REACH):
         near = jnp.where(inside & (g_lane - g_row == d), own_filter[d : d + 1], near)
-    mm[:, 256:384] = near
+    put_mm(2, near)
+    sub8 = iota((8, 128), 0)
+    for h in range(2):
+        span = own_rates[h] * float(STRETCH)
+        for i, d in enumerate((1, 2, 4)):
+            powers[h, 8 * i : 8 * i + 8, :] = jnp.where(sub8 >= d, jnp.exp(-span * float(d)), 0.0)
+        powers[h, 24:32, :] = jnp.exp(-span * (sub8 + 1).astype(F32))
+        powers[h, 32:40, :] = jnp.broadcast_to(jnp.exp(-span * 8.0), (8, 128))
+        powers[h, 40:41, :] = jnp.exp(-own_rates[h] * float(STRETCH - REACH))
+        powers[h, 41:42, :] = jnp.exp(-own_rates[h] * float(REACH))
+        powers[h, 42:43, :] = own_amounts[h]
 
     def halves(x):
         hi = jnp.floor(x * (1.0 / 256.0))
@@ -429,21 +415,26 @@
 
     def put(kind, rows, x):
         hi, lo = halves(x)
-        at = pl.ds(kind * 128 + rows, x.shape[0])
-        codes_s[at, 0:128] = hi.astype(BF16)
-        codes_s[at, 128:256] = lo.astype(BF16)
+        at = pl.ds(rows, x.shape[0])
+        codes_s[at, kind * 256 : kind * 256 + 128] = hi.astype(BF16)
+        codes_s[at, kind * 256 + 128 : kind * 256 + 256] = lo.astype(BF16)
 
     all_of(send_b, recv_b, 0).wait_recv()
     recv_to_stage(recv_b, 8, 0, widen)
-    rows_s[...] = jnp.dot(pb[...], stage[...].astype(BF16), preferred_element_type=F32)
+    raw = jnp.concatenate(
+        [stage[pl.ds(kind, SLOTS, stride=4), :].astype(BF16) for kind in range(4)], axis=1
+    )
+    rows_s[0:128, 0:256] = jnp.dot(gather[0:128, :], raw[:, 0:256], preferred_element_type=F32)
+    rows_s[128:256, :] = jnp.dot(gather[128:256, :], raw, preferred_element_type=F32)
     group = iota((16, 128), 1) >> 4
 
-    @pl.loop(0, 8)
+    @pl.loop(0, 8, unroll=2)
     def _(b):
         first = pl.multiple_of(b * 16, 16)
 
-        def block(kind):
-            return rows_s[pl.ds(pl.multiple_of(kind * 128 + b * 16, 16), 16), :]
+        def block(kind, before):
+            at = pl.ds(pl.multiple_of(before * 128 + b * 16, 16), 16)
+            return rows_s[at, kind * 128 : kind * 128 + 128]
 
         def edge(head, tail, taps):
             total = taps[0:1] * head
@@ -453,56 +444,54 @@
             return total
 
         rows = pl.ds(first, 16)
-        head_v, tail_k, tail_v = block(1), block(2), block(3)
-        six[rows, :] = edge(block(0), tail_k, taps_k) * edge(head_v, tail_v, taps_v)
+        head_v, tail_k, tail_v = block(1, 0), block(2, 1), block(3, 1)
+        six[rows, :] = edge(block(0, 0), tail_k, taps_k) * edge(head_v, tail_v, taps_v)
         scale = jnp.where(group == 6, head_v * (1.0 / FULL), 0.0)
         for shift in (16, 32, 64):
             scale = scale + pltpu.roll(scale, shift, 1)
         scale_s[rows, :] = scale
         tail_q = jnp.where(group >= 4, pltpu.roll(tail_v, 64, 1), pltpu.roll(tail_k, 32, 1))
-        tail_q = jnp.where(group >= 6, block(4), tail_q)
+        tail_q = jnp.where(group >= 6, block(0, 1), tail_q)
         part = edge(jnp.zeros_like(tail_q), tail_q, taps_q)
         part = jnp.where(group < REACH, part, 0.0)
         power = power_of(group_max(jnp.abs(part)))
         put(3, first, jnp.where(group == 6, power, encode(part, power)))
 
-    extra[...] = jnp.dot(six[...], mm[...], precision=HIGHEST, preferred_element_type=F32)
+    upper, lower = split(six[...])
+    wide = jnp.concatenate([upper, upper, lower], axis=1)
+    extra[...] = jnp.dot(wide, mm[...], preferred_element_type=F32)
 
     all_of(send_e, recv_e, 1).wait_recv()
     recv_to_stage(recv_e, 4, 0, uncode)
-    hi, lo = halves(stage[0:256, :])
-    both = jnp.concatenate([hi.astype(BF16), lo.astype(BF16)], axis=1)
-    both = jnp.dot(pe[...], both, preferred_element_type=F32)
-    codes = both[:, :128] * 256.0 + both[:, 128:]
-    sub8 = iota((8, 128), 0)
+    parts = []
+    for h in range(2):
+        parts += [x.astype(BF16) for x in halves(stage[pl.ds(h, SLOTS, stride=2), :])]
+    both = jnp.concatenate(parts, axis=1)
+    both = jnp.dot(gather[0:128, :], both, preferred_element_type=F32)
     for h in range(2):
         lanes = slice(128 * h, 128 * h + 128)
-        late = jnp.exp(-own_rates[h] * float(STRETCH - REACH))
-        x = codes[128 * h : 128 * h + 128] * scale_s[...] + extra[:, lanes] * late
-        span = own_rates[h] * float(STRETCH)
+        codes = both[:, 256 * h : 256 * h + 128] * 256.0 + both[:, 256 * h + 128 : 256 * h + 256]
+        x = codes * scale_s[...] + extra[:, lanes] * powers[h, 40:41, :]
         blocks = [x[8 * b : 8 * b + 8] for b in range(16)]
-        for d in (1, 2, 4):
-            mult = jnp.where(sub8 >= d, jnp.exp(-span * float(d)), 0.0)
+        for i, d in enumerate((1, 2, 4)):
+            mult = powers[h, 8 * i : 8 * i + 8, :]
             blocks = [x + mult * pltpu.roll(x, d, 0) for x in blocks]
-        lift = jnp.exp(-span * (sub8 + 1).astype(F32))
-        whole = jnp.broadcast_to(jnp.exp(-span * 8.0), (8, 128))
+        lift, whole = powers[h, 24:32, :], powers[h, 32:40, :]
         carry = jnp.zeros((8, 128), F32)
         scan_s[h, 0:8, :] = carry
         for b in range(16):
             total = jnp.broadcast_to(blocks[b][7:8], (8, 128))
             scan_s[h, 8 * b + 1 : 8 * b + 9, :] = blocks[b] + lift * carry
             carry = whole * carry + total
-    start = [scan_s[h, 0:128, :] * own_amounts[h] for h in range(2)]
-    wide = jnp.concatenate(start, axis=1)
-    upper = wide.astype(BF16)
-    lower = (wide - upper.astype(F32)).astype(BF16)
+    start = [scan_s[h, 0:128, :] * powers[h, 42:43, :] for h in range(2)]
+    upper, lower = split(jnp.concatenate(start, axis=1))
     wide = jnp.concatenate([upper, upper, lower], axis=1)
-    rows_s[0:128, :] = extra[:, 256:384] + jnp.dot(
+    rows_s[0:128, 0:128] = extra[:, 256:384] + jnp.dot(
         wide, m1[...], preferred_element_type=F32
     )
     late = [
-        start[h] * jnp.exp(-own_rates[h] * float(REACH))
-        + extra[:, 128 * h : 128 * h + 128] * own_amounts[h]
+        start[h] * powers[h, 41:42, :]
+        + extra[:, 128 * h : 128 * h + 128] * powers[h, 42:43, :]
         for h in range(2)
     ]
     for b in range(8):
@@ -512,12 +501,15 @@
         )
         for h in range(2):
             put(h, 16 * b, encode(late[h][rows], power))
-        y = rows_s[rows, :]
+        y = rows_s[rows, 0:128]
         power_y = power_of(group_max(jnp.abs(y)))
         y = jnp.where(group == 6, power, jnp.where(group == 7, power_y, encode(y, power_y)))
         put(2, 16 * b, y)
-    both = jnp.dot(qs[...], codes_s[...], preferred_element_type=F32)
-    stage[...] = both[:, :128] * 256.0 + both[:, 128:]
+    both = jnp.dot(scatter[...], codes_s[...], preferred_element_type=F32)
+    for kind in range(4):
+        hi = both[:, 256 * kind : 256 * kind + 128]
+        lo = both[:, 256 * kind + 128 : 256 * kind + 256]
+        stage[pl.ds(kind, SLOTS, stride=4), :] = hi * 256.0 + lo
     stage_to_send(send_s, 8, 0, code)
     send_all(send_s, recv_s, 2)
     recv_s[me] = send_s[me]
@@ -650,9 +642,9 @@
         + [f32(TOKENS, WIDTH)]
         + [f32(ORDER * 8, 128)] * 2
         + [f32(192, 128), f32((STRETCH + PAD) * 8, 128), f32(512, 128), f32(64, 128), f32(128, 128)]
-        + [bf16(640, 512), bf16(256, 256), bf16(512, 512)]
-        + [f32(128, 384), bf16(768, 128), f32(128, 384), f32(640, 128), bf16(512, 256)]
-        + [f32(2, 136, 128), f32(128, 128), f32(512, 128), f32(128, 128)]
+        + [bf16(256, 128), bf16(128, 128), f32(2, 48, 128)]
+        + [bf16(384, 384), bf16(768, 128), f32(128, 384), f32(256, 512), bf16(128, 1024)]
+        + [f32(2, 136, 128), f32(128, 128), f32(128, 128)]
         + [bf16(OWNERS, 8, 128)] * 2
         + [i16(OWNERS, 4, 128)] * 2
         + [i16(OWNERS, 8, 128)] * 2
@@ -662,7 +654,7 @@
     )
     return pl.pallas_call(
         functools.partial(kernel, n_ch, width_all),
-        out_shape=jax.ShapeDtypeStruct((TOKENS, WIDTH), BF16),
+        out_shape=pltpu.VMEM((TOKENS, WIDTH), BF16),
         in_specs=[hbm] * 9,
         out_specs=vmem,
         scratch_shapes=scratch,

time: 52.5 us -> 50.4 us (0.960)
  Pallas kernels: 50.6 us -> 49.6 us
  local copies, waits for them, and re-layouts: 1.67 us -> 0.71 us
    pallas_call x1, Pallas kernels: 50.6 us -> 49.6 us  [on_device(): pl.pallas_call(functools.partial(kernel, n_ch, width_all), out_shape=pltp...]
    unnamed x1, local copies, waits for them, and re-layouts: 1.67 us -> 0.71 us
where the time goes in v4:
time: 50.4 us; the launch traced here: 50.3 us
  Pallas kernels  49.6 us (98%)
  local copies, waits for them, and re-layouts  0.71 us (1%)
    pallas_call x1, Pallas kernels, on_device(): pl.pallas_call(functools.partial(kernel, n_ch, width_all), out_shape=pltp...  49.6 us

profile of v4, /device:TPU:1, one launch (start us, length us, event | category | flops | bytes accessed | tf_op | source)
XLA Modules:
  0.0 50.3 jit_solution(4701282396295586522)
XLA Ops:
  0.0 49.6 %hyena.1 = bf16[128,1024]{1,0:T(8,128)(2,1)S(1)} custom-call(bf16[128,1024]{1,0:T(8,128)(2,1)} %q_hbm.1, bf16[128,1024]{1,0:T(8,128)(2,1)} %k_hbm.1, bf16[128,1024]{1,0:T(8,128)(2,1)} %v_hbm.1, s32[1,128]{1,0:T(1,128)} %bitcast.5, f32[3,7,1024]{2,1,0:T(8,128)} %sw_hbm.1, f32[16,1024]{1,0:T(8,128)} %rates_hbm.1, f32[16,1024]{1,0:T(8,128)} %res_hbm.1, ...), custom_call_target="tpu_custom_call" | custom-call | tf_op jit(solution)/shard_map/hyena/pallas_call | solution.py:655
  49.6 0.7 %copy.11 = bf16[128,1024]{1,0:T(8,128)(2,1)} copy(bf16[128,1024]{1,0:T(8,128)(2,1)S(1)} %hyena.1) | data formatting | bytes 524288

commit v5 on v4

--- a/solution.py
+++ b/solution.py
@@ -10,7 +10,6 @@
 F32 = jnp.float32
 BF16 = jnp.bfloat16
 MESH = pl.DeviceIdType.MESH
-HIGHEST = lax.Precision.HIGHEST
 
 TOKENS = 128
 WIDTH = 1024
@@ -116,11 +115,19 @@
 
     barrier = pltpu.get_barrier_semaphore()
 
-    @pl.loop(1, OWNERS)
+    def peer_z(step):
+        return (my_z + (2 * (step % 2) - 1) * ((step + 1) // 2) + 16) % 16
+
+    def greet(d):
+        pl.semaphore_signal(barrier, 1, device_id={"ctx": d}, device_id_type=MESH)
+
+    @pl.loop(0, 15)
     def _(i):
-        pl.semaphore_signal(
-            barrier, 1, device_id={"ctx": (me + i) % OWNERS}, device_id_type=MESH
-        )
+        for l in range(4):
+            greet(peer_z(15 - i) * 4 + l)
+
+    for l in range(1, 4):
+        greet(my_z * 4 + (my_l + l) % 4)
 
     @pl.loop(1, n_ch)
     def _(i):
@@ -145,27 +152,24 @@
         "gain": load(8, gain_hbm, gain_ref),
     }
 
+    def send_one(src, dst, sem, d):
+        pltpu.make_async_remote_copy(
+            src_ref=src.at[d],
+            dst_ref=dst.at[me],
+            send_sem=ssem.at[sem],
+            recv_sem=rsem.at[sem],
+            device_id={"ctx": d},
+            device_id_type=MESH,
+        ).start()
+
     def send_all(src, dst, sem):
-        def one(d):
-            pltpu.make_async_remote_copy(
-                src_ref=src.at[d],
-                dst_ref=dst.at[me],
-                send_sem=ssem.at[sem],
-                recv_sem=rsem.at[sem],
-                device_id={"ctx": d},
-                device_id_type=MESH,
-            ).start()
-
         @pl.loop(0, 15)
         def _(i):
-            step = 15 - i
-            far = (step + 1) // 2
-            d_z = (my_z + (2 * (step % 2) - 1) * far + 16) % 16
             for l in range(4):
-                one(d_z * 4 + (my_l + l) % 4)
+                send_one(src, dst, sem, peer_z(15 - i) * 4 + (my_l + l) % 4)
 
         for l in range(1, 4):
-            one(my_z * 4 + (my_l + l) % 4)
+            send_one(src, dst, sem, my_z * 4 + (my_l + l) % 4)
 
     def all_of(src, dst, sem):
         return pltpu.make_async_remote_copy(
@@ -562,9 +566,11 @@
             z_s[rows, :] = z_s[rows, :] * (y_s[rows, :] + sums[0])
             return state
 
-        lax.fori_loop(
-            REACH, STRETCH, last, tuple(x * scale for x in low + high), unroll=2
+        state = lax.fori_loop(
+            REACH, STRETCH - 2, last, tuple(x * scale for x in low + high), unroll=4
         )
+        for t in (STRETCH - 2, STRETCH - 1):
+            state = last(t, state)
 
     @pl.loop(0, 16)
     def _(b):
@@ -572,19 +578,19 @@
         total = jnp.zeros((8, 128), F32)
         for j in range(8):
             z = z_s[pl.ds(b * 64 + j, 8, stride=8), :]
-            zn_s[rows, 128 * j : 128 * j + 128] = z
+            lanes = slice(128 * j, 128 * j + 128)
+            zn_s[rows, lanes] = z * gain_ref[:, lanes]
             total = total + z * z
         sq_s[rows, :] = total
 
     sums = lax.dot_general(
-        jnp.ones((8, 128), F32),
-        sq_s[...],
+        jnp.ones((8, 256), BF16),
+        jnp.concatenate(split(sq_s[...]), axis=1),
         (((1,), (1,)), ((), ())),
-        precision=HIGHEST,
         preferred_element_type=F32,
     )
-    sq_send[0] = sums
-    sq_recv[my_ch] = sums
+    sq_send[0] = sums[0:1]
+    sq_recv[my_ch] = sums[0:1]
 
     @pl.loop(1, n_ch)
     def _(i):
@@ -610,7 +616,7 @@
     for i in range(1, n_ch):
         total = total + sq_recv[i]
     scale = lax.rsqrt(total / float(width_all) + EPS)
-    sq_s[...] = jnp.transpose(jnp.broadcast_to(scale[0:1], (128, 128)))
+    sq_s[...] = jnp.transpose(jnp.broadcast_to(scale, (128, 128)))
 
     @pl.loop(0, 8)
     def _(b):
@@ -618,7 +624,7 @@
         by = sq_s[rows, :]
         for j in range(8):
             lanes = slice(128 * j, 128 * j + 128)
-            o_ref[rows, lanes] = (zn_s[rows, lanes] * by * gain_ref[:, lanes]).astype(BF16)
+            o_ref[rows, lanes] = (zn_s[rows, lanes] * by).astype(BF16)
 
     all_of(send_b, recv_b, 0).wait_send()
     all_of(send_e, recv_e, 1).wait_send()
@@ -648,7 +654,7 @@
         + [bf16(OWNERS, 8, 128)] * 2
         + [i16(OWNERS, 4, 128)] * 2
         + [i16(OWNERS, 8, 128)] * 2
-        + [f32(1, 8, 128), f32(n_ch, 8, 128)]
+        + [f32(1, 1, 128), f32(n_ch, 1, 128)]
         + [pltpu.SemaphoreType.DMA((4,)), pltpu.SemaphoreType.DMA((4,))]
         + [pltpu.SemaphoreType.DMA((9,))]
     )

time: 50.4 us -> 49.1 us (0.974)
  Pallas kernels: 49.6 us -> 48.3 us
    pallas_call x1, Pallas kernels: 49.6 us -> 48.3 us  [on_device(): pl.pallas_call(functools.partial(kernel, n_ch, width_all), out_shape=pltp...]
where the time goes in v5:
time: 49.1 us; the launch traced here: 49 us
  Pallas kernels  48.3 us (98%)
  local copies, waits for them, and re-layouts  0.71 us (1%)
    pallas_call x1, Pallas kernels, on_device(): pl.pallas_call(functools.partial(kernel, n_ch, width_all), out_shape=pltp...  48.3 us

profile of v5, /device:TPU:1, one launch (start us, length us, event | category | flops | bytes accessed | tf_op | source)
XLA Modules:
  0.0 49.0 jit_solution(5078156552968647332)
XLA Ops:
  0.0 48.3 %hyena.1 = bf16[128,1024]{1,0:T(8,128)(2,1)S(1)} custom-call(bf16[128,1024]{1,0:T(8,128)(2,1)} %q_hbm.1, bf16[128,1024]{1,0:T(8,128)(2,1)} %k_hbm.1, bf16[128,1024]{1,0:T(8,128)(2,1)} %v_hbm.1, s32[1,128]{1,0:T(1,128)} %bitcast.5, f32[3,7,1024]{2,1,0:T(8,128)} %sw_hbm.1, f32[16,1024]{1,0:T(8,128)} %rates_hbm.1, f32[16,1024]{1,0:T(8,128)} %res_hbm.1, ...), custom_call_target="tpu_custom_call" | custom-call | tf_op jit(solution)/shard_map/hyena/pallas_call | solution.py:661
  48.3 0.7 %copy.11 = bf16[128,1024]{1,0:T(8,128)(2,1)} copy(bf16[128,1024]{1,0:T(8,128)(2,1)S(1)} %hyena.1) | data formatting | bytes 524288

commit v6 on v5

--- a/solution.py
+++ b/solution.py
@@ -83,6 +83,7 @@
     sw,
     filt,
     stage,
+    stage_e,
     own,
     six,
     gather,
@@ -162,14 +163,16 @@
             device_id_type=MESH,
         ).start()
 
-    def send_all(src, dst, sem):
+    def send_all(*sets):
         @pl.loop(0, 15)
         def _(i):
             for l in range(4):
-                send_one(src, dst, sem, peer_z(15 - i) * 4 + (my_l + l) % 4)
+                for one in sets:
+                    send_one(*one, peer_z(15 - i) * 4 + (my_l + l) % 4)
 
         for l in range(1, 4):
-            send_one(src, dst, sem, my_z * 4 + (my_l + l) % 4)
+            for one in sets:
+                send_one(*one, my_z * 4 + (my_l + l) % 4)
 
     def all_of(src, dst, sem):
         return pltpu.make_async_remote_copy(
@@ -193,7 +196,7 @@
     def widen(x):
         return x.astype(F32)
 
-    def stage_to_send(dst, pitch, first, convert):
+    def stage_to_send(dst, pitch, first, convert, stage=stage):
         rows = dst.shape[1]
 
         @pl.loop(0, 8)
@@ -202,7 +205,7 @@
                 d = b * 8 + i
                 dst[d] = convert(stage[pl.ds(d * pitch + first, rows), :])
 
-    def recv_to_stage(src, pitch, first, convert):
+    def recv_to_stage(src, pitch, first, convert, stage=stage):
         rows = src.shape[1]
 
         @pl.loop(0, 8)
@@ -299,8 +302,7 @@
     stage_to_send(send_b, 8, 0, narrow)
 
     pl.semaphore_wait(barrier, OWNERS - 1 + n_ch - 1)
-    send_all(send_b, recv_b, 0)
-    send_all(send_e, recv_e, 1)
+    send_all((send_b, recv_b, 0), (send_e, recv_e, 1))
     recv_b[me] = send_b[me]
     recv_e[me] = send_e[me]
 
@@ -425,6 +427,8 @@
 
     all_of(send_b, recv_b, 0).wait_recv()
     recv_to_stage(recv_b, 8, 0, widen)
+    all_of(send_e, recv_e, 1).wait_recv()
+    recv_to_stage(recv_e, 4, 0, uncode, stage_e)
     raw = jnp.concatenate(
         [stage[pl.ds(kind, SLOTS, stride=4), :].astype(BF16) for kind in range(4)], axis=1
     )
@@ -432,12 +436,11 @@
     rows_s[128:256, :] = jnp.dot(gather[128:256, :], raw, preferred_element_type=F32)
     group = iota((16, 128), 1) >> 4
 
-    @pl.loop(0, 8, unroll=2)
-    def _(b):
-        first = pl.multiple_of(b * 16, 16)
+    for b in range(8):
+        first = b * 16
 
         def block(kind, before):
-            at = pl.ds(pl.multiple_of(before * 128 + b * 16, 16), 16)
+            at = pl.ds(before * 128 + b * 16, 16)
             return rows_s[at, kind * 128 : kind * 128 + 128]
 
         def edge(head, tail, taps):
@@ -465,11 +468,9 @@
     wide = jnp.concatenate([upper, upper, lower], axis=1)
     extra[...] = jnp.dot(wide, mm[...], preferred_element_type=F32)
 
-    all_of(send_e, recv_e, 1).wait_recv()
-    recv_to_stage(recv_e, 4, 0, uncode)
     parts = []
     for h in range(2):
-        parts += [x.astype(BF16) for x in halves(stage[pl.ds(h, SLOTS, stride=2), :])]
+        parts += [x.astype(BF16) for x in halves(stage_e[pl.ds(h, SLOTS, stride=2), :])]
     both = jnp.concatenate(parts, axis=1)
     both = jnp.dot(gather[0:128, :], both, preferred_element_type=F32)
     for h in range(2):
@@ -515,7 +516,7 @@
         lo = both[:, 256 * kind + 128 : 256 * kind + 256]
         stage[pl.ds(kind, SLOTS, stride=4), :] = hi * 256.0 + lo
     stage_to_send(send_s, 8, 0, code)
-    send_all(send_s, recv_s, 2)
+    send_all((send_s, recv_s, 2))
     recv_s[me] = send_s[me]
 
     for b in range(8):
@@ -647,7 +648,7 @@
         + [f32(TOKENS * 8, 128)] * 3
         + [f32(TOKENS, WIDTH)]
         + [f32(ORDER * 8, 128)] * 2
-        + [f32(192, 128), f32((STRETCH + PAD) * 8, 128), f32(512, 128), f32(64, 128), f32(128, 128)]
+        + [f32(192, 128), f32((STRETCH + PAD) * 8, 128), f32(512, 128), f32(256, 128), f32(64, 128), f32(128, 128)]
         + [bf16(256, 128), bf16(128, 128), f32(2, 48, 128)]
         + [bf16(384, 384), bf16(768, 128), f32(128, 384), f32(256, 512), bf16(128, 1024)]
         + [f32(2, 136, 128), f32(128, 128), f32(128, 128)]

time: 49.1 us -> 47.8 us (0.974)
  Pallas kernels: 48.3 us -> 47 us
    pallas_call x1, Pallas kernels: 48.3 us -> 47 us  [on_device(): pl.pallas_call(functools.partial(kernel, n_ch, width_all), out_shape=pltp...]
where the time goes in v6:
time: 47.8 us; the launch traced here: 47.7 us
  Pallas kernels  47 us (98%)
  local copies, waits for them, and re-layouts  0.71 us (1%)
    pallas_call x1, Pallas kernels, on_device(): pl.pallas_call(functools.partial(kernel, n_ch, width_all), out_shape=pltp...  47 us

profile of v6, /device:TPU:1, one launch (start us, length us, event | category | flops | bytes accessed | tf_op | source)
XLA Modules:
  0.0 47.7 jit_solution(8714260680576617961)
XLA Ops:
  0.0 47.0 %hyena.1 = bf16[128,1024]{1,0:T(8,128)(2,1)S(1)} custom-call(bf16[128,1024]{1,0:T(8,128)(2,1)} %q_hbm.1, bf16[128,1024]{1,0:T(8,128)(2,1)} %k_hbm.1, bf16[128,1024]{1,0:T(8,128)(2,1)} %v_hbm.1, s32[1,128]{1,0:T(1,128)} %bitcast.5, f32[3,7,1024]{2,1,0:T(8,128)} %sw_hbm.1, f32[16,1024]{1,0:T(8,128)} %rates_hbm.1, f32[16,1024]{1,0:T(8,128)} %res_hbm.1, ...), custom_call_target="tpu_custom_call" | custom-call | tf_op jit(solution)/shard_map/hyena/pallas_call | solution.py:662
  47.0 0.7 %copy.11 = bf16[128,1024]{1,0:T(8,128)(2,1)} copy(bf16[128,1024]{1,0:T(8,128)(2,1)S(1)} %hyena.1) | data formatting | bytes 524288

commit v7 on v6

--- a/solution.py
+++ b/solution.py
@@ -168,7 +168,7 @@
         def _(i):
             for l in range(4):
                 for one in sets:
-                    send_one(*one, peer_z(15 - i) * 4 + (my_l + l) % 4)
+                    send_one(*one, peer_z(15 - i) * 4 + ((my_l // 2) * 2 + 2 + l) % 4)
 
         for l in range(1, 4):
             for one in sets:
@@ -573,16 +573,18 @@
         for t in (STRETCH - 2, STRETCH - 1):
             state = last(t, state)
 
-    @pl.loop(0, 16)
+    @pl.loop(0, 16, unroll=4)
     def _(b):
         rows = pl.ds(pl.multiple_of(b * 8, 8), 8)
-        total = jnp.zeros((8, 128), F32)
+        squares = []
         for j in range(8):
             z = z_s[pl.ds(b * 64 + j, 8, stride=8), :]
             lanes = slice(128 * j, 128 * j + 128)
             zn_s[rows, lanes] = z * gain_ref[:, lanes]
-            total = total + z * z
-        sq_s[rows, :] = total
+            squares.append(z * z)
+        while len(squares) > 1:
+            squares = [x + y for x, y in zip(squares[0::2], squares[1::2])]
+        sq_s[rows, :] = squares[0]
 
     sums = lax.dot_general(
         jnp.ones((8, 256), BF16),
@@ -619,7 +621,7 @@
     scale = lax.rsqrt(total / float(width_all) + EPS)
     sq_s[...] = jnp.transpose(jnp.broadcast_to(scale, (128, 128)))
 
-    @pl.loop(0, 8)
+    @pl.loop(0, 8, unroll=2)
     def _(b):
         rows = pl.ds(pl.multiple_of(b * 16, 16), 16)
         by = sq_s[rows, :]

time: 47.8 us -> 47.5 us (level)
  no operation moved by 1% of the time
where the time goes in v7:
time: 47.5 us; the launch traced here: 47.4 us
  Pallas kernels  46.7 us (98%)
  local copies, waits for them, and re-layouts  0.71 us (1%)
    pallas_call x1, Pallas kernels, on_device(): pl.pallas_call(functools.partial(kernel, n_ch, width_all), out_shape=pltp...  46.7 us

profile of v7, /device:TPU:1, one launch (start us, length us, event | category | flops | bytes accessed | tf_op | source)
XLA Modules:
  0.0 47.4 jit_solution(1099899665719045375)
XLA Ops:
  0.0 46.7 %hyena.1 = bf16[128,1024]{1,0:T(8,128)(2,1)S(1)} custom-call(bf16[128,1024]{1,0:T(8,128)(2,1)} %q_hbm.1, bf16[128,1024]{1,0:T(8,128)(2,1)} %k_hbm.1, bf16[128,1024]{1,0:T(8,128)(2,1)} %v_hbm.1, s32[1,128]{1,0:T(1,128)} %bitcast.5, f32[3,7,1024]{2,1,0:T(8,128)} %sw_hbm.1, f32[16,1024]{1,0:T(8,128)} %rates_hbm.1, f32[16,1024]{1,0:T(8,128)} %res_hbm.1, ...), custom_call_target="tpu_custom_call" | custom-call | tf_op jit(solution)/shard_map/hyena/pallas_call | solution.py:664
  46.7 0.7 %copy.11 = bf16[128,1024]{1,0:T(8,128)(2,1)} copy(bf16[128,1024]{1,0:T(8,128)(2,1)S(1)} %hyena.1) | data formatting | bytes 524288
